TPU v7x, 1024 devices: a whole 4x4x32 slice. The times are simulated.
1024 devices in a mesh: gx: 64 (over z, y_lo), gz: 4 (over x), ta: 4 (over y_hi, core).
Axes of the slice: x: 4, y: 4 (y_hi: 2, y_lo: 2; y = y_hi * 2 + y_lo), z: 32, core: 2. Of those that a mesh axis runs over, the one named last changes fastest.
Arguments:
- rhs: float32 [64, 2, 2, 16, 16, 8, 64], P('gx', None, None, 'gz', 'ta'), may hold values from -20 to 20
- self_coupling: bfloat16 [64, 2, 2, 16, 16, 64, 64], P('gx', None, None, 'gz', 'ta'), may hold values from -0.75 to 0.75
- hopping: bfloat16 [4, 64, 2, 2, 16, 16, 64, 64], P(None, 'gx', None, None, 'gz', 'ta'), may hold values from -0.5 to 0.5
Outputs:
- solution: float32 [64, 2, 2, 16, 16, 8, 64], P('gx', None, None, 'gz', 'ta')
- residual: float32 [64, 2, 2, 16, 16, 8, 64], P('gx', None, None, 'gz', 'ta')
All inputs are finite; a program needn't handle non-finite values.
Results may differ from a plain program's by a relative error of at most 0.0087.
Values may be sent and summed in bfloat16 or wider, within the bound.
A program may use at most 32 MiB of HBM per device.

v0:
```python
import jax
import jax.numpy as jnp
from jax import lax
from jax.sharding import PartitionSpec as P

MR_STEPS = 2


def passed_along(block, axis, distance):
    devices = range(lax.axis_size(axis))
    route = [((i - distance) % len(devices), i) for i in devices]
    return lax.ppermute(block, axis, route)


def site_product(link_block, field_bf):
    return jnp.einsum(
        "xyztab,xyztrb->xyztra", link_block, field_bf, preferred_element_type=jnp.float32
    )


def site_product_back(link_block, field_bf):
    return jnp.einsum(
        "xyztab,xyztra->xyztrb", link_block, field_bf, preferred_element_type=jnp.float32
    )


def rim(values, along, position):
    return lax.slice_in_dim(values, position, position + 1, axis=along)


def plane_move(rim_face, offset):
    return passed_along(rim_face, "gx", offset)


def depth_move(rim_face, offset):
    return passed_along(rim_face, "gz", offset)


def time_move(rim_face, offset):
    return passed_along(rim_face, "ta", offset)


def neighbour_rim(rim_face, direction, toward, row_len):
    if direction == 0:
        return plane_move(rim_face, -toward * row_len)
    if direction == 1:
        return plane_move(rim_face, -toward)
    if direction == 2:
        return depth_move(rim_face, -toward)
    return time_move(rim_face, -toward)


def local_dot(left, right):
    return jnp.sum(left * right, axis=(0, 1, 2, 3, 5))[:, None]


def mesh_total(partials):
    return lax.psum(partials, ("gx", "gz", "ta"))


def on_device(rhs, self_coupling, hopping):
    source = rhs[0]
    self_links = self_coupling[0]
    hop_links = hopping[:, 0]
    channels = source.shape[5]
    chirality = jnp.where(jnp.arange(channels) < channels // 2, 1.0, -1.0).astype(jnp.bfloat16)
    row_len = min(8, max(2, lax.axis_size("gx") // 8))
    link_rims = []
    for direction in range(4):
        last_index = hop_links.shape[direction + 1] - 1
        link_rims.append(
            neighbour_rim(rim(hop_links[direction], direction, last_index), direction, -1, row_len)
        )

    def apply_operator(vector, reach):
        field_bf = vector.astype(jnp.bfloat16)
        result = 4.0 * vector + site_product(self_links, field_bf)
        flipped = chirality * field_bf
        for direction in range(4):
            link_block = hop_links[direction]
            extent = vector.shape[direction]
            back_term = (chirality * site_product_back(link_block, flipped)).astype(jnp.bfloat16)
            if reach == "local":
                upper_rim = jnp.zeros_like(rim(field_bf, direction, 0))
                lower_rim = jnp.zeros_like(rim(back_term, direction, 0))
            else:
                upper_rim = neighbour_rim(rim(field_bf, direction, 0), direction, 1, row_len)
                below_rim = neighbour_rim(
                    rim(field_bf, direction, extent - 1), direction, -1, row_len
                )
                lower_rim = (
                    chirality * site_product_back(link_rims[direction], chirality * below_rim)
                ).astype(jnp.bfloat16)
            ahead_field = jnp.concatenate(
                [lax.slice_in_dim(field_bf, 1, extent, axis=direction), upper_rim], axis=direction
            )
            behind = jnp.concatenate(
                [lower_rim, lax.slice_in_dim(back_term, 0, extent - 1, axis=direction)],
                axis=direction,
            )
            result = result + site_product(link_block, ahead_field) + behind.astype(jnp.float32)
        return result

    def smoothing(start_field):
        remain = start_field
        update = jnp.zeros_like(start_field)
        for repeat_index in range(MR_STEPS):
            mapped = apply_operator(remain, "local")
            weight = local_dot(mapped, remain) / local_dot(mapped, mapped)
            update = update + weight * remain
            remain = remain - weight * mapped
        return update

    direction_zero = smoothing(source)
    mapped_zero = apply_operator(direction_zero, "global")
    first_sums = mesh_total(
        jnp.stack([local_dot(mapped_zero, source), local_dot(mapped_zero, mapped_zero)])
    )
    alpha_first = first_sums[0] / first_sums[1]
    solution_one = alpha_first * direction_zero
    residual_one = source - alpha_first * mapped_zero
    direction_raw = smoothing(residual_one)
    mapped_raw = apply_operator(direction_raw, "global")
    orth_sums = mesh_total(jnp.stack([local_dot(mapped_zero, mapped_raw)]))
    beta_value = orth_sums[0] / first_sums[1]
    direction_one = direction_raw - beta_value * direction_zero
    mapped_one = mapped_raw - beta_value * mapped_zero
    last_sums = mesh_total(
        jnp.stack([local_dot(mapped_one, residual_one), local_dot(mapped_one, mapped_one)])
    )
    alpha_second = last_sums[0] / last_sums[1]
    solution = solution_one + alpha_second * direction_one
    residual = residual_one - alpha_second * mapped_one
    return (solution[None], residual[None])


def solution(mesh):
    in_specs = (
        P("gx", None, None, "gz", "ta", None, None),
        P("gx", None, None, "gz", "ta", None, None),
        P(None, "gx", None, None, "gz", "ta", None, None),
    )
    out_specs = (
        P("gx", None, None, "gz", "ta", None, None),
        P("gx", None, None, "gz", "ta", None, None),
    )
    return jax.shard_map(
        on_device, mesh=mesh, in_specs=in_specs, out_specs=out_specs, check_vma=False
    )
```

profile of v0, /device:TPU:1, one launch (start us, length us, event | category | flops | bytes accessed | tf_op | source)
XLA Modules:
  0.0 644.7 jit_solution(11878094864844023320)
XLA Ops:
  0.7 2.7 slice_bitcast_fusion
  3.4 6.2 collective-permute-start.11
  20.2 1.9 collective-permute-start.10
  22.2 11.7 %collective-permute-start.9 = (bf16[2,2,4,1,8,64]{5,4,3,2,1,0:T(8,128)(2,1)S(1)}, bf16[2,2,4,1,8,64]{5,4,3,2,1,0:T(8,128)(2,1)S(1)}, u32[]{:S(2)}, u32[]{:S(2)}) collective-permute-start(bf16[2,2,4,1,8,64]{5,4,3,2,1,0:T(8,128)(2,1)S(1)} %get-tuple-element.37), channel_id=1, source_target_pairs={{1,0},{2,1},{3,2},{0,3},{5,4},{6,5},{7,6},{4,7},{9,8},{10,9},{11,1... | collective-permute-start | bytes 49160 | tf_op jit(solution)/shard_map/ppermute | solution.py:12
  33.9 1.9 collective-permute-start.8
  35.9 4.6 collective-permute-start.6
  42.9 1.9 collective-permute-start.5
  45.5 9.2 %collective-permute-start.3 = (bf16[2,1,4,4,8,64]{5,4,3,2,1,0:T(8,128)(2,1)S(1)}, bf16[2,1,4,4,8,64]{5,4,3,2,1,0:T(8,128)(2,1)S(1)}, u32[]{:S(2)}, u32[]{:S(2)}) collective-permute-start(bf16[2,1,4,4,8,64]{5,4,3,2,1,0:T(8,128)(2,1)S(1)} %get-tuple-element.43), channel_id=1, source_target_pairs={{16,0},{32,16},{48,32},{64,48},{80,64},{96,80},{112,96},{128,112},... | collective-permute-start | bytes 98312 | tf_op jit(solution)/shard_map/ppermute | solution.py:12
  58.6 1.9 collective-permute-start.7
  60.5 5.7 collective-permute-start.2
  66.4 8.8 %collective-permute-start.1 = (bf16[1,2,4,4,8,64]{5,4,3,2,1,0:T(8,128)(2,1)S(1)}, bf16[1,2,4,4,8,64]{5,4,3,2,1,0:T(8,128)(2,1)S(1)}, u32[]{:S(2)}, u32[]{:S(2)}) collective-permute-start(bf16[1,2,4,4,8,64]{5,4,3,2,1,0:T(8,128)(2,1)S(1)} %get-tuple-element.40), channel_id=1, source_target_pairs={{896,0},{912,16},{928,32},{944,48},{960,64},{976,80},{992,96},{100... | collective-permute-start | bytes 98312 | tf_op jit(solution)/shard_map/ppermute | solution.py:12
  75.2 7.7 %collective-permute-start = (bf16[1,2,4,4,8,64]{5,4,3,2,1,0:T(8,128)(2,1)S(1)}, bf16[1,2,4,4,8,64]{5,4,3,2,1,0:T(8,128)(2,1)S(1)}, u32[]{:S(2)}, u32[]{:S(2)}) collective-permute-start(bf16[1,2,4,4,8,64]{5,4,3,2,1,0:T(8,128)(2,1)S(1)} %get-tuple-element.41), channel_id=1, source_target_pairs={{128,0},{144,16},{160,32},{176,48},{192,64},{208,80},{224,96},{240... | collective-permute-start | bytes 98312 | tf_op jit(solution)/shard_map/ppermute | solution.py:12
  83.4 28.4 %collective-permute-done.1 = bf16[1,2,4,4,8,64]{5,4,3,2,1,0:T(8,128)(2,1)S(1)} collective-permute-done((bf16[1,2,4,4,8,64]{5,4,3,2,1,0:T(8,128)(2,1)S(1)}, bf16[1,2,4,4,8,64]{5,4,3,2,1,0:T(8,128)(2,1)S(1)}, u32[]{:S(2)}, u32[]{:S(2)}) %collective-permute-start.1) | collective-permute-done | bytes 32800 | tf_op jit(solution)/shard_map/ppermute | solution.py:12
  112.9 173.0 %psum.21 = f32[2,8,1]{1,2,0:T(1,128)S(1)} all-reduce(f32[2,8,1]{1,2,0:T(1,128)S(1)} %pad_maximum_fusion), channel_id=1, replica_groups=mesh['gx'=64,'gz'=4,'ta'=4] {'gx','gz','ta'}, use_global_device_ids=true, to_apply=%region_6.7 | all-reduce | flops 16 | bytes 128 | tf_op jit(solution)/shard_map/psum | solution.py:58
  301.9 3.6 collective-permute-start.19
  305.5 1.9 collective-permute-start.18
  307.5 1.9 collective-permute-start.17
  309.4 4.6 collective-permute-start.16
  314.0 1.9 collective-permute-start.15
  316.6 5.5 collective-permute-start.14
  322.8 2.8 collective-permute-start.13
  326.2 6.4 collective-permute-start.12
  335.9 155.4 %psum.22 = f32[1,8,1]{1,2,0:T(1,128)S(1)} all-reduce(f32[1,8,1]{1,2,0:T(1,128)S(1)} %bitcast.204), channel_id=1, replica_groups=mesh['gx'=64,'gz'=4,'ta'=4] {'gx','gz','ta'}, use_global_device_ids=true, to_apply=%region_12.13 | all-reduce | flops 8 | bytes 64 | tf_op jit(solution)/shard_map/psum | solution.py:58
  491.6 152.1 %psum.23 = f32[2,8,1]{1,2,0:T(1,128)S(1)} all-reduce(f32[2,8,1]{1,2,0:T(1,128)S(1)} %pad_maximum_fusion.1), channel_id=1, replica_groups=mesh['gx'=64,'gz'=4,'ta'=4] {'gx','gz','ta'}, use_global_device_ids=true, to_apply=%region_15.16 | all-reduce | flops 16 | bytes 128 | tf_op jit(solution)/shard_map/psum | solution.py:58
  (152 shorter events, 41.6 us)
Async XLA Ops:
  0.6 10.6 %copy-start = (bf16[1,2,2,4,4,64,64]{6,5,4,3,2,1,0:T(8,128)(2,1)S(1)}, bf16[1,2,2,4,4,64,64]{6,5,4,3,2,1,0:T(8,128)(2,1)}, u32[]{:S(2)}) copy-start(bf16[1,2,2,4,4,64,64]{6,5,4,3,2,1,0:T(8,128)(2,1)} %param.4) | copy-start | bytes 1572868
  0.6 9.1 %copy-start.1 = (bf16[4,1,2,2,4,4,64,64]{7,6,5,4,3,2,1,0:T(8,128)(2,1)S(1)}, bf16[4,1,2,2,4,4,64,64]{7,6,5,4,3,2,1,0:T(8,128)(2,1)}, u32[]{:S(2)}) copy-start(bf16[4,1,2,2,4,4,64,64]{7,6,5,4,3,2,1,0:T(8,128)(2,1)} %param.5) | copy-start | bytes 6291460
  3.4 57.1 %collective-permute-start.11 = (bf16[2,2,4,1,64,64]{5,4,3,2,1,0:T(8,128)(2,1)S(1)}, bf16[2,2,4,1,64,64]{5,4,3,2,1,0:T(8,128)(2,1)S(1)}, u32[]{:S(2)}, u32[]{:S(2)}) collective-permute-start(bf16[2,2,4,1,64,64]{5,4,3,2,1,0:T(8,128)(2,1)S(1)} %slice.357), channel_id=1, source_target_pairs={{3,0},{0,1},{1,2},{2,3},{7,4},{4,5},{5,6},{6,7},{11,8},{8,9},{9,10... | collective-permute-start | bytes 393224 | tf_op jit(solution)/shard_map/ppermute | solution.py:12
  20.2 38.3 %collective-permute-start.10 = (bf16[2,2,4,1,8,64]{5,4,3,2,1,0:T(8,128)(2,1)S(1)}, bf16[2,2,4,1,8,64]{5,4,3,2,1,0:T(8,128)(2,1)S(1)}, u32[]{:S(2)}, u32[]{:S(2)}) collective-permute-start(bf16[2,2,4,1,8,64]{5,4,3,2,1,0:T(8,128)(2,1)S(1)} %get-tuple-element.36), channel_id=1, source_target_pairs={{3,0},{0,1},{1,2},{2,3},{7,4},{4,5},{5,6},{6,7},{11,8},{8,9},{9,10... | collective-permute-start | bytes 49160 | tf_op jit(solution)/shard_map/ppermute | solution.py:12
  22.2 20.8 %collective-permute-start.9 = (bf16[2,2,4,1,8,64]{5,4,3,2,1,0:T(8,128)(2,1)S(1)}, bf16[2,2,4,1,8,64]{5,4,3,2,1,0:T(8,128)(2,1)S(1)}, u32[]{:S(2)}, u32[]{:S(2)}) collective-permute-start(bf16[2,2,4,1,8,64]{5,4,3,2,1,0:T(8,128)(2,1)S(1)} %get-tuple-element.37), channel_id=1, source_target_pairs={{1,0},{2,1},{3,2},{0,3},{5,4},{6,5},{7,6},{4,7},{9,8},{10,9},{11,1... | collective-permute-start | bytes 49160 | tf_op jit(solution)/shard_map/ppermute | solution.py:12
  33.9 41.3 %collective-permute-start.8 = (bf16[2,2,1,4,64,64]{5,4,3,2,1,0:T(8,128)(2,1)S(1)}, bf16[2,2,1,4,64,64]{5,4,3,2,1,0:T(8,128)(2,1)S(1)}, u32[]{:S(2)}, u32[]{:S(2)}) collective-permute-start(bf16[2,2,1,4,64,64]{5,4,3,2,1,0:T(8,128)(2,1)S(1)} %slice.352), channel_id=1, source_target_pairs={{12,0},{0,4},{4,8},{8,12},{13,1},{1,5},{5,9},{9,13},{14,2},{2,6},{... | collective-permute-start | bytes 393224 | tf_op jit(solution)/shard_map/ppermute | solution.py:12
  35.9 9.6 %collective-permute-start.6 = (bf16[2,2,1,4,8,64]{5,4,3,2,1,0:T(8,128)(2,1)S(1)}, bf16[2,2,1,4,8,64]{5,4,3,2,1,0:T(8,128)(2,1)S(1)}, u32[]{:S(2)}, u32[]{:S(2)}) collective-permute-start(bf16[2,2,1,4,8,64]{5,4,3,2,1,0:T(8,128)(2,1)S(1)} %get-tuple-element.39), channel_id=1, source_target_pairs={{4,0},{8,4},{12,8},{0,12},{5,1},{9,5},{13,9},{1,13},{6,2},{10,6},{... | collective-permute-start | bytes 49160 | tf_op jit(solution)/shard_map/ppermute | solution.py:12
  42.9 40.2 %collective-permute-start.5 = (bf16[2,1,4,4,64,64]{5,4,3,2,1,0:T(8,128)(2,1)S(1)}, bf16[2,1,4,4,64,64]{5,4,3,2,1,0:T(8,128)(2,1)S(1)}, u32[]{:S(2)}, u32[]{:S(2)}) collective-permute-start(bf16[2,1,4,4,64,64]{5,4,3,2,1,0:T(8,128)(2,1)S(1)} %slice.347), channel_id=1, source_target_pairs={{1008,0},{0,16},{16,32},{32,48},{48,64},{64,80},{80,96},{96,112},{... | collective-permute-start | bytes 786440 | tf_op jit(solution)/shard_map/ppermute | solution.py:12
  45.5 10.5 %collective-permute-start.3 = (bf16[2,1,4,4,8,64]{5,4,3,2,1,0:T(8,128)(2,1)S(1)}, bf16[2,1,4,4,8,64]{5,4,3,2,1,0:T(8,128)(2,1)S(1)}, u32[]{:S(2)}, u32[]{:S(2)}) collective-permute-start(bf16[2,1,4,4,8,64]{5,4,3,2,1,0:T(8,128)(2,1)S(1)} %get-tuple-element.43), channel_id=1, source_target_pairs={{16,0},{32,16},{48,32},{64,48},{80,64},{96,80},{112,96},{128,112},... | collective-permute-start | bytes 98312 | tf_op jit(solution)/shard_map/ppermute | solution.py:12
  56.0 27.1 %collective-permute-start.4 = (bf16[2,1,4,4,8,64]{5,4,3,2,1,0:T(8,128)(2,1)S(1)}, bf16[2,1,4,4,8,64]{5,4,3,2,1,0:T(8,128)(2,1)S(1)}, u32[]{:S(2)}, u32[]{:S(2)}) collective-permute-start(bf16[2,1,4,4,8,64]{5,4,3,2,1,0:T(8,128)(2,1)S(1)} %get-tuple-element.42), channel_id=1, source_target_pairs={{1008,0},{0,16},{16,32},{32,48},{48,64},{64,80},{80,96},{96,112},{... | collective-permute-start | bytes 98312 | tf_op jit(solution)/shard_map/ppermute | solution.py:12
  58.6 7.8 %collective-permute-start.7 = (bf16[2,2,1,4,8,64]{5,4,3,2,1,0:T(8,128)(2,1)S(1)}, bf16[2,2,1,4,8,64]{5,4,3,2,1,0:T(8,128)(2,1)S(1)}, u32[]{:S(2)}, u32[]{:S(2)}) collective-permute-start(bf16[2,2,1,4,8,64]{5,4,3,2,1,0:T(8,128)(2,1)S(1)} %get-tuple-element.38), channel_id=1, source_target_pairs={{12,0},{0,4},{4,8},{8,12},{13,1},{1,5},{5,9},{9,13},{14,2},{2,6},{... | collective-permute-start | bytes 49160 | tf_op jit(solution)/shard_map/ppermute | solution.py:12
  60.5 51.3 %collective-permute-start.2 = (bf16[1,2,4,4,64,64]{5,4,3,2,1,0:T(8,128)(2,1)S(1)}, bf16[1,2,4,4,64,64]{5,4,3,2,1,0:T(8,128)(2,1)S(1)}, u32[]{:S(2)}, u32[]{:S(2)}) collective-permute-start(bf16[1,2,4,4,64,64]{5,4,3,2,1,0:T(8,128)(2,1)S(1)} %slice_bitcast_fusion.3), channel_id=1, source_target_pairs={{896,0},{912,16},{928,32},{944,48},{960,64},{976,80},{992,96},{100... | collective-permute-start | bytes 786440 | tf_op jit(solution)/shard_map/ppermute | solution.py:12
  66.4 45.4 %collective-permute-start.1 = (bf16[1,2,4,4,8,64]{5,4,3,2,1,0:T(8,128)(2,1)S(1)}, bf16[1,2,4,4,8,64]{5,4,3,2,1,0:T(8,128)(2,1)S(1)}, u32[]{:S(2)}, u32[]{:S(2)}) collective-permute-start(bf16[1,2,4,4,8,64]{5,4,3,2,1,0:T(8,128)(2,1)S(1)} %get-tuple-element.40), channel_id=1, source_target_pairs={{896,0},{912,16},{928,32},{944,48},{960,64},{976,80},{992,96},{100... | collective-permute-start | bytes 98312 | tf_op jit(solution)/shard_map/ppermute | solution.py:12
  75.2 210.7 %copy-start.4 = (bf16[2,2,1,4,64,64]{5,4,3,2,1,0:T(8,128)(2,1)}, bf16[2,2,1,4,64,64]{5,4,3,2,1,0:T(8,128)(2,1)S(1)}, u32[]{:S(2)}) copy-start(bf16[2,2,1,4,64,64]{5,4,3,2,1,0:T(8,128)(2,1)S(1)} %collective-permute-done.8) | copy-start | bytes 393220
  75.2 36.8 %collective-permute-start = (bf16[1,2,4,4,8,64]{5,4,3,2,1,0:T(8,128)(2,1)S(1)}, bf16[1,2,4,4,8,64]{5,4,3,2,1,0:T(8,128)(2,1)S(1)}, u32[]{:S(2)}, u32[]{:S(2)}) collective-permute-start(bf16[1,2,4,4,8,64]{5,4,3,2,1,0:T(8,128)(2,1)S(1)} %get-tuple-element.41), channel_id=1, source_target_pairs={{128,0},{144,16},{160,32},{176,48},{192,64},{208,80},{224,96},{240... | collective-permute-start | bytes 98312 | tf_op jit(solution)/shard_map/ppermute | solution.py:12
  301.5 31.3 %copy-start.5 = (bf16[2,2,1,4,64,64]{5,4,3,2,1,0:T(8,128)(2,1)S(1)}, bf16[2,2,1,4,64,64]{5,4,3,2,1,0:T(8,128)(2,1)}, u32[]{:S(2)}) copy-start(bf16[2,2,1,4,64,64]{5,4,3,2,1,0:T(8,128)(2,1)} %copy-done.4) | copy-start | bytes 393220
  301.9 24.3 %collective-permute-start.19 = (bf16[2,2,4,1,8,64]{5,4,3,2,1,0:T(8,128)(2,1)S(1)}, bf16[2,2,4,1,8,64]{5,4,3,2,1,0:T(8,128)(2,1)S(1)}, u32[]{:S(2)}, u32[]{:S(2)}) collective-permute-start(bf16[2,2,4,1,8,64]{5,4,3,2,1,0:T(8,128)(2,1)S(1)} %get-tuple-element.28), channel_id=1, source_target_pairs={{3,0},{0,1},{1,2},{2,3},{7,4},{4,5},{5,6},{6,7},{11,8},{8,9},{9,10... | collective-permute-start | bytes 49160 | tf_op jit(solution)/shard_map/ppermute | solution.py:12
  305.5 11.1 %collective-permute-start.18 = (bf16[2,2,4,1,8,64]{5,4,3,2,1,0:T(8,128)(2,1)S(1)}, bf16[2,2,4,1,8,64]{5,4,3,2,1,0:T(8,128)(2,1)S(1)}, u32[]{:S(2)}, u32[]{:S(2)}) collective-permute-start(bf16[2,2,4,1,8,64]{5,4,3,2,1,0:T(8,128)(2,1)S(1)} %get-tuple-element.29), channel_id=1, source_target_pairs={{1,0},{2,1},{3,2},{0,3},{5,4},{6,5},{7,6},{4,7},{9,8},{10,9},{11,1... | collective-permute-start | bytes 49160 | tf_op jit(solution)/shard_map/ppermute | solution.py:12
  307.5 25.3 %collective-permute-start.17 = (bf16[2,2,1,4,8,64]{5,4,3,2,1,0:T(8,128)(2,1)S(1)}, bf16[2,2,1,4,8,64]{5,4,3,2,1,0:T(8,128)(2,1)S(1)}, u32[]{:S(2)}, u32[]{:S(2)}) collective-permute-start(bf16[2,2,1,4,8,64]{5,4,3,2,1,0:T(8,128)(2,1)S(1)} %get-tuple-element.30), channel_id=1, source_target_pairs={{12,0},{0,4},{4,8},{8,12},{13,1},{1,5},{5,9},{9,13},{14,2},{2,6},{... | collective-permute-start | bytes 49160 | tf_op jit(solution)/shard_map/ppermute | solution.py:12
  309.4 13.4 %collective-permute-start.16 = (bf16[2,2,1,4,8,64]{5,4,3,2,1,0:T(8,128)(2,1)S(1)}, bf16[2,2,1,4,8,64]{5,4,3,2,1,0:T(8,128)(2,1)S(1)}, u32[]{:S(2)}, u32[]{:S(2)}) collective-permute-start(bf16[2,2,1,4,8,64]{5,4,3,2,1,0:T(8,128)(2,1)S(1)} %get-tuple-element.31), channel_id=1, source_target_pairs={{4,0},{8,4},{12,8},{0,12},{5,1},{9,5},{13,9},{1,13},{6,2},{10,6},{... | collective-permute-start | bytes 49160 | tf_op jit(solution)/shard_map/ppermute | solution.py:12
  314.0 19.6 %collective-permute-start.15 = (bf16[2,1,4,4,8,64]{5,4,3,2,1,0:T(8,128)(2,1)S(1)}, bf16[2,1,4,4,8,64]{5,4,3,2,1,0:T(8,128)(2,1)S(1)}, u32[]{:S(2)}, u32[]{:S(2)}) collective-permute-start(bf16[2,1,4,4,8,64]{5,4,3,2,1,0:T(8,128)(2,1)S(1)} %get-tuple-element.34), channel_id=1, source_target_pairs={{1008,0},{0,16},{16,32},{32,48},{48,64},{64,80},{80,96},{96,112},{... | collective-permute-start | bytes 98312 | tf_op jit(solution)/shard_map/ppermute | solution.py:12
  316.6 16.4 %collective-permute-start.14 = (bf16[2,1,4,4,8,64]{5,4,3,2,1,0:T(8,128)(2,1)S(1)}, bf16[2,1,4,4,8,64]{5,4,3,2,1,0:T(8,128)(2,1)S(1)}, u32[]{:S(2)}, u32[]{:S(2)}) collective-permute-start(bf16[2,1,4,4,8,64]{5,4,3,2,1,0:T(8,128)(2,1)S(1)} %get-tuple-element.35), channel_id=1, source_target_pairs={{16,0},{32,16},{48,32},{64,48},{80,64},{96,80},{112,96},{128,112},... | collective-permute-start | bytes 98312 | tf_op jit(solution)/shard_map/ppermute | solution.py:12
  322.8 11.2 %collective-permute-start.13 = (bf16[1,2,4,4,8,64]{5,4,3,2,1,0:T(8,128)(2,1)S(1)}, bf16[1,2,4,4,8,64]{5,4,3,2,1,0:T(8,128)(2,1)S(1)}, u32[]{:S(2)}, u32[]{:S(2)}) collective-permute-start(bf16[1,2,4,4,8,64]{5,4,3,2,1,0:T(8,128)(2,1)S(1)} %get-tuple-element.32), channel_id=1, source_target_pairs={{896,0},{912,16},{928,32},{944,48},{960,64},{976,80},{992,96},{100... | collective-permute-start | bytes 98312 | tf_op jit(solution)/shard_map/ppermute | solution.py:12
  326.2 9.0 %collective-permute-start.12 = (bf16[1,2,4,4,8,64]{5,4,3,2,1,0:T(8,128)(2,1)S(1)}, bf16[1,2,4,4,8,64]{5,4,3,2,1,0:T(8,128)(2,1)S(1)}, u32[]{:S(2)}, u32[]{:S(2)}) collective-permute-start(bf16[1,2,4,4,8,64]{5,4,3,2,1,0:T(8,128)(2,1)S(1)} %get-tuple-element.33), channel_id=1, source_target_pairs={{128,0},{144,16},{160,32},{176,48},{192,64},{208,80},{224,96},{240... | collective-permute-start | bytes 98312 | tf_op jit(solution)/shard_map/ppermute | solution.py:12
  (2 other events, 14.1 us)
where the time goes:
time: 646 us; the launch traced here: 645 us
  blocking collectives  480 us (74%)
  starting transfers between devices  92.1 us (14%)
  matrix products  35.3 us (5%)
  waiting for transfers between devices  30 us (5%)
    psum x3, blocking collectives, mesh_total(): return lax.psum(partials, ('gx', 'gz', 'ta'))  480 us
    ppermute x20, starting transfers between devices, passed_along(): return lax.ppermute(block, axis, route)  92.1 us
    ppermute x20, waiting for transfers between devices, passed_along(): return lax.ppermute(block, axis, route)  30 us
    dot_general x30, matrix products, site_product(): jnp.einsum('xyztab,xyztrb->xyztra', link_block, field_bf, preferred_eleme...  20.4 us
    dot_general x32, matrix products, site_product_back(): jnp.einsum('xyztab,xyztra->xyztrb', link_block, field_bf, preferred_eleme...  14.8 us
  transfers between devices with their start and end apart: 20, of which 3 were waited for; matrix products, arithmetic and copies ran while one was open for 3% of the time, Pallas kernels for 0%

commit v1 on v0

v1 whole, which is shorter than its diff:
```python
import functools

import jax
import jax.numpy as jnp
from jax import lax
from jax.experimental import pallas as pl
from jax.experimental.pallas import tpu as pltpu
from jax.sharding import PartitionSpec as P

MESH = pl.DeviceIdType.MESH
EXT = (2, 2, 4, 4)
F32 = jnp.float32
BF16 = jnp.bfloat16
STAGES = (7, 3, 3, 8)
SLOTS = sum(STAGES)


def part(direction, low, high):
    return tuple(slice(low, high) if d == direction else slice(None) for d in range(4))


def flat(values):
    return values.reshape((-1,) + values.shape[4:])


def forward_dot(fields, links):
    return lax.dot_general(fields, links, (((2,), (2,)), ((0,), (0,))), preferred_element_type=F32)


def backward_dot(fields, links):
    return lax.dot_general(fields, links, (((2,), (1,)), ((0,), (0,))), preferred_element_type=F32)


def whole(mesh_size, value):
    return lax.rem(value + mesh_size, mesh_size)


class Place:
    def __init__(self, sizes, row_len):
        self.sizes = sizes
        self.row_len = row_len
        self.gx = lax.axis_index("gx")
        self.gz = lax.axis_index("gz")
        self.ta = lax.axis_index("ta")

    def at(self, gx=0, gz=0, ta=0, flip_gx=0, flip_ta=0):
        x = whole(self.sizes["gx"], self.gx + gx)
        z = whole(self.sizes["gz"], self.gz + gz)
        t = whole(self.sizes["ta"], self.ta + ta)
        if flip_gx:
            x = x + 1 - 2 * lax.rem(x, 2)
        if flip_ta & 1:
            t = t + 1 - 2 * lax.rem(t, 2)
        if flip_ta & 2:
            t = whole(self.sizes["ta"], t + 2)
        return {"gx": x, "gz": z, "ta": t}

    def ahead(self, direction, sign):
        if direction == 0:
            return self.at(gx=sign * self.row_len)
        if direction == 1:
            return self.at(gx=sign)
        if direction == 2:
            return self.at(gz=sign)
        return self.at(ta=sign)

    def stage(self, index):
        if index == 0:
            out = [self.at(gz=k, flip_ta=c) for k in range(4) for c in range(2)]
            return out[1:]
        if index == 1:
            return [self.at(flip_gx=1), self.at(flip_ta=2), self.at(flip_gx=1, flip_ta=2)]
        if index == 2:
            return [self.at(gx=2), self.at(gx=-2), self.at(gx=-4)]
        return [self.at(gx=2 * k) for k in (2, -2, 6, -6, 10, -10, 14, -14)]


def on_device(sizes, row_len, rhs_hbm, self_hbm, hop_hbm, sol_ref, res_ref,
              rhs, links, hops, vb, vc, acc_f, acc_b, m0, m1, r1, d0, z_field, rt, lt, lz,
              lt2, lz2, d1, send_xy, send_zt, got_xy, got_zt, rows_out, rows_in,
              load_sem, halo_send, halo_recv, sum_send, sum_recv):
    place = Place(sizes, row_len)
    loads = [pltpu.make_async_copy(rhs_hbm, rhs, load_sem.at[0]),
             pltpu.make_async_copy(self_hbm, links, load_sem.at[1])]
    for d in range(4):
        loads.append(pltpu.make_async_copy(hop_hbm.at[d], hops.at[d], load_sem.at[2 + d]))
    for load in loads:
        load.start()

    greeted = [place.ahead(d, sign) for d in range(4) for sign in (1, -1)]
    greeted += place.stage(0) + place.stage(1) + [place.at(gx=2), place.at(gx=-2)] + place.stage(3)
    barrier = pltpu.get_barrier_semaphore()
    for other in greeted:
        pl.semaphore_signal(barrier, inc=1, device_id=other, device_id_type=MESH)

    lane = lax.broadcasted_iota(jnp.int32, (1, 1, 64), 2)
    chi = jnp.where(lane < 32, 1.0, -1.0).astype(F32)
    lane_r = lax.broadcasted_iota(jnp.int32, (8, 128), 1)
    sub_r = lax.broadcasted_iota(jnp.int32, (8, 128), 0)

    def dot_sum(a, b):
        return jnp.sum(jnp.sum(flat(a) * flat(b), axis=0), axis=-1, keepdims=True)

    def to_row(columns):
        spread = jnp.zeros((8, 128), F32)
        for k, column in enumerate(columns):
            spread = jnp.where(lane_r == 8 * k + sub_r, column, spread)
        return jnp.sum(spread, axis=0, keepdims=True)

    def from_row(row, k):
        return jnp.sum(jnp.where(lane_r == 8 * k + sub_r, row, 0.0), axis=1, keepdims=True)

    def load_fields(fields):
        pieces = []
        for field in fields:
            top = field.astype(BF16).astype(F32)
            pieces += [top, field - top]
        stacked = jnp.concatenate(pieces, axis=4)
        height = 16 * len(fields)
        vb[..., 0:height, :] = stacked.astype(BF16)
        vc[..., 0:height, :] = (stacked * chi).astype(BF16)
        return height

    def local_apply(fields, outs, first=False):
        h = load_fields(fields)
        if first:
            loads[1].wait()
        acc_f[..., 0:h, :] = forward_dot(flat(vb[..., 0:h, :]), flat(links[...])).reshape(EXT + (h, 64))
        acc_b[..., 0:h, :] = jnp.zeros(EXT + (h, 64), F32)
        for d in range(4):
            if first:
                loads[2 + d].wait()
            low, high = part(d, 0, EXT[d] - 1), part(d, 1, EXT[d])
            block = flat(hops[(d,) + low])
            shape = tuple(EXT[k] - (k == d) for k in range(4)) + (h, 64)
            span = (slice(0, h), slice(None))
            acc_f[low + span] += forward_dot(flat(vb[high + span]), block).reshape(shape)
            acc_b[high + span] += backward_dot(flat(vc[low + span]), block).reshape(shape)
        for k, (field, out) in enumerate(zip(fields, outs)):
            a, b = slice(16 * k, 16 * k + 8), slice(16 * k + 8, 16 * k + 16)
            total_f = acc_f[..., a, :] + acc_f[..., b, :]
            total_b = acc_b[..., a, :] + acc_b[..., b, :]
            out[...] = 4.0 * field + total_f + chi * total_b

    def face_refs(store, around, d, kind):
        xy, zt = store
        return (xy if d < 2 else zt).at[around, d % 2, kind]

    def pack(face):
        half = face.shape[0] // 2
        return jnp.concatenate([face[:half], face[half:]], axis=-1).astype(BF16)

    def unpack(ref):
        both = ref[...].astype(F32)
        return jnp.concatenate([both[..., :64], both[..., 64:]], axis=0)

    def halo_copy(around, d, kind):
        slot = (around * 4 + d) * 2 + kind
        return pltpu.make_async_remote_copy(
            src_ref=face_refs((send_xy, send_zt), around, d, kind),
            dst_ref=face_refs((got_xy, got_zt), around, d, kind),
            send_sem=halo_send.at[slot],
            recv_sem=halo_recv.at[slot],
            device_id=place.ahead(d, -1 if kind == 0 else 1),
            device_id_type=MESH,
        )

    def halo_start(around, field):
        for d in range(4):
            low = flat(field[part(d, 0, 1)])
            face_refs((send_xy, send_zt), around, d, 0)[...] = pack(low)
            halo_copy(around, d, 0).start()
            top = part(d, EXT[d] - 1, EXT[d])
            flipped = (flat(field[top]) * chi).astype(BF16)
            back = chi * backward_dot(flipped, flat(hops[(d,) + top]))
            face_refs((send_xy, send_zt), around, d, 1)[...] = pack(back)
            halo_copy(around, d, 1).start()

    def halo_finish(around, out):
        for d in (2, 3, 1, 0):
            shape = tuple(1 if k == d else EXT[k] for k in range(4)) + (8, 64)
            halo_copy(around, d, 0).wait_recv()
            top = part(d, EXT[d] - 1, EXT[d])
            ahead = unpack(face_refs((got_xy, got_zt), around, d, 0)).astype(BF16)
            out[top] += forward_dot(ahead, flat(hops[(d,) + top])).reshape(shape)
            halo_copy(around, d, 1).wait_recv()
            low = part(d, 0, 1)
            out[low] += unpack(face_refs((got_xy, got_zt), around, d, 1)).reshape(shape)

    def sum_copies(around, index):
        base = around * SLOTS + sum(STAGES[:index])
        return [
            pltpu.make_async_remote_copy(
                src_ref=rows_out.at[around * 4 + index],
                dst_ref=rows_in.at[base + k],
                send_sem=sum_send.at[base + k],
                recv_sem=sum_recv.at[base + k],
                device_id=other,
                device_id_type=MESH,
            )
            for k, other in enumerate(place.stage(index))
        ]

    def sum_start(around, index, row):
        rows_out[around * 4 + index] = row
        copies = sum_copies(around, index)
        for copy in copies:
            copy.start()
        return copies

    def sum_finish(around, index, copies, row):
        base = around * SLOTS + sum(STAGES[:index])
        total = row
        for k, copy in enumerate(copies):
            copy.wait_recv()
            got = rows_in[base + k]
            total = got if total is None else total + got
        return total

    def mesh_sum(around, row, meanwhile=None):
        for index in range(4):
            copies = sum_start(around, index, row)
            kept = row if index < 3 else None
            if index == 3 and meanwhile is not None:
                meanwhile()
            row = sum_finish(around, index, copies, kept)
        return row

    loads[0].wait()
    source = rhs[...]
    local_apply([source], [m0], first=True)
    first = m0[...]
    source = rhs[...]
    weight_a = dot_sum(first, source) / dot_sum(first, first)
    r1[...] = source - weight_a * first
    local_apply([r1[...]], [m1])
    second, left = m1[...], r1[...]
    weight_b = dot_sum(second, left) / dot_sum(second, second)
    d0[...] = weight_a * rhs[...] + weight_b * left
    pl.semaphore_wait(barrier, len(greeted))
    halo_start(0, d0)
    z_field[...] = weight_a * m0[...] + weight_b * m1[...]
    halo_finish(0, z_field)

    zero = z_field[...]
    part_zr, part_zz = dot_sum(zero, rhs[...]), dot_sum(zero, zero)
    centre = jnp.where(part_zz > 0.0, part_zr / jnp.where(part_zz > 0.0, part_zz, 1.0), 0.0)

    def meanwhile():
        rt[...] = rhs[...] - centre * z_field[...]
        local_apply([rt[...], z_field[...]], [lt, lz])
        local_apply([lt[...], lz[...]], [lt2, lz2])

    sums = mesh_sum(0, to_row([part_zr, part_zz]), meanwhile)
    sum_zz = from_row(sums, 1)
    alpha = from_row(sums, 0) / sum_zz
    shift = alpha - centre
    r1[...] = rhs[...] - alpha * z_field[...]
    m0[...] = lt[...] - shift * lz[...]
    first = m0[...]
    weight_a = dot_sum(first, r1[...]) / dot_sum(first, first)
    m1[...] = m0[...] - weight_a * (lt2[...] - shift * lz2[...])
    rt[...] = r1[...] - weight_a * m0[...]
    second = m1[...]
    weight_b = dot_sum(second, rt[...]) / dot_sum(second, second)
    d1[...] = weight_a * r1[...] + weight_b * rt[...]
    halo_start(1, d1)
    lz[...] = weight_a * m0[...] + weight_b * m1[...]
    halo_finish(1, lz)

    raw = lz[...]
    columns = [dot_sum(z_field[...], raw), dot_sum(raw, r1[...]), dot_sum(raw, raw),
               dot_sum(z_field[...], r1[...])]
    sums = mesh_sum(1, to_row(columns))
    cross, onto, square, kept = [from_row(sums, k) for k in range(4)]
    beta = cross / sum_zz
    alpha_b = (onto - beta * kept) / (square - beta * (2.0 * cross - beta * sum_zz))
    sol_ref[...] = alpha * d0[...] + alpha_b * (d1[...] - beta * d0[...])
    res_ref[...] = r1[...] - alpha_b * (lz[...] - beta * z_field[...])

    for around in range(2):
        for d in range(4):
            for kind in range(2):
                halo_copy(around, d, kind).wait_send()
        for index in range(4):
            for copy in sum_copies(around, index):
                copy.wait_send()


def solution(mesh):
    sizes = dict(mesh.shape)
    row_len = min(8, max(2, sizes["gx"] // 8))

    def step(rhs, self_coupling, hopping):
        field = EXT + (8, 64)
        vmem = pl.BlockSpec(memory_space=pltpu.VMEM)
        hbm = pl.BlockSpec(memory_space=pl.ANY)
        fields = [pltpu.VMEM(field, F32)] * 10
        sol, res = pl.pallas_call(
            functools.partial(on_device, sizes, row_len),
            out_shape=[jax.ShapeDtypeStruct(field, F32)] * 2,
            in_specs=[hbm] * 3,
            out_specs=[vmem] * 2,
            scratch_shapes=[
                pltpu.VMEM(field, F32),
                pltpu.VMEM(EXT + (64, 64), BF16),
                pltpu.VMEM((4,) + EXT + (64, 64), BF16),
                pltpu.VMEM(EXT + (32, 64), BF16),
                pltpu.VMEM(EXT + (32, 64), BF16),
                pltpu.VMEM(EXT + (32, 64), F32),
                pltpu.VMEM(EXT + (32, 64), F32),
                *fields,
                pltpu.VMEM(field, F32),
                pltpu.VMEM((2, 2, 2, 16, 8, 128), BF16),
                pltpu.VMEM((2, 2, 2, 8, 8, 128), BF16),
                pltpu.VMEM((2, 2, 2, 16, 8, 128), BF16),
                pltpu.VMEM((2, 2, 2, 8, 8, 128), BF16),
                pltpu.VMEM((8, 1, 128), F32),
                pltpu.VMEM((2 * SLOTS, 1, 128), F32),
                pltpu.SemaphoreType.DMA((6,)),
                pltpu.SemaphoreType.DMA((16,)),
                pltpu.SemaphoreType.DMA((16,)),
                pltpu.SemaphoreType.DMA((2 * SLOTS,)),
                pltpu.SemaphoreType.DMA((2 * SLOTS,)),
            ],
            compiler_params=pltpu.CompilerParams(collective_id=0, has_side_effects=True),
        )(rhs[0], self_coupling[0], hopping[:, 0])
        return sol[None], res[None]

    whole_spec = P("gx", None, None, "gz", "ta", None, None)
    return jax.shard_map(
        step,
        mesh=mesh,
        in_specs=(whole_spec, whole_spec, P(None, "gx", None, None, "gz", "ta", None, None)),
        out_specs=(whole_spec, whole_spec),
        check_vma=False,
    )
```

time: 646 us -> 90.9 us (0.14)
  blocking collectives: 480 us -> 0 us
  starting transfers between devices: 92.1 us -> 0 us
  Pallas kernels: 0 us -> 85.5 us
  matrix products: 35.3 us -> 0 us
  waiting for transfers between devices: 30 us -> 0 us
    psum x3 -> x0, blocking collectives: 480 us -> none  [mesh_total(): return lax.psum(partials, ('gx', 'gz', 'ta'))]
    ppermute x20 -> x0, starting transfers between devices: 92.1 us -> none  [passed_along(): return lax.ppermute(block, axis, route)]
    pallas_call x0 -> x1, Pallas kernels: none -> 85.5 us  [step(): pl.pallas_call(functools.partial(on_device, sizes, row_len), out_shape=[j...]
    dot_general x62 -> x0, matrix products: 35.3 us -> none  [the longest x30 20.4 us: site_product(): jnp.einsum('xyztab,xyztrb->xyztra', link_block, field_bf, preferred_eleme...]
    ppermute x20 -> x0, waiting for transfers between devices: 30 us -> none  [passed_along(): return lax.ppermute(block, axis, route)]
  transfers between devices with their start and end apart: 20 -> 0, of which waited for: 3 -> 0; matrix products, arithmetic and copies ran while one was open for 3% -> 0% of each run, Pallas kernels for 0% -> 0%
where the time goes in v1:
time: 90.9 us; the launch traced here: 89.5 us
  Pallas kernels  85.5 us (94%)
  local copies, waits for them, and re-layouts  3.34 us (4%)
    pallas_call x1, Pallas kernels, step(): pl.pallas_call(functools.partial(on_device, sizes, row_len), out_shape=[j...  85.5 us
    unnamed x2, local copies, waits for them, and re-layouts  3.34 us

profile of v1, /device:TPU:1, one launch (start us, length us, event | category | flops | bytes accessed | tf_op | source)
XLA Modules:
  0.0 89.5 jit_solution(13465975671215656933)
XLA Ops:
  0.6 85.5 %shard_map.50 = (f32[2,2,4,4,8,64]{5,4,3,2,1,0:T(8,128)}, f32[2,2,4,4,8,64]{5,4,3,2,1,0:T(8,128)}) custom-call(f32[2,2,4,4,8,64]{5,4,3,2,1,0:T(8,128)} %bitcast.9, bf16[2,2,4,4,64,64]{5,4,3,2,1,0:T(8,128)(2,1)} %bitcast.6, bf16[4,2,2,4,4,64,64]{6,5,4,3,2,1,0:T(8,128)(2,1)} %bitcast.5), custom_call_target="tpu_custom_call" | custom-call | tf_op jit(solution)/shard_map/pallas_call | solution.py:299
  86.2 1.7 %copy.7 = f32[1,2,2,4,4,8,64]{6,5,4,3,2,1,0:T(8,128)} copy(f32[1,2,2,4,4,8,64]{6,5,4,3,2,1,0:T(8,128)} %bitcast.8) | data formatting | bytes 262144
  87.9 1.7 %copy.8 = f32[1,2,2,4,4,8,64]{6,5,4,3,2,1,0:T(8,128)} copy(f32[1,2,2,4,4,8,64]{6,5,4,3,2,1,0:T(8,128)} %bitcast.7) | data formatting | bytes 262144

commit v2 on v1

v2 whole, which is shorter than its diff:
```python
import functools

import jax
import jax.numpy as jnp
from jax import lax
from jax.experimental import pallas as pl
from jax.experimental.pallas import tpu as pltpu
from jax.sharding import PartitionSpec as P

MESH = pl.DeviceIdType.MESH
EXT = (2, 2, 4, 4)
F32 = jnp.float32
BF16 = jnp.bfloat16
STAGES = (1, 15, 31)
SLOTS = sum(STAGES)


def part(direction, low, high):
    return tuple(slice(low, high) if d == direction else slice(None) for d in range(4))


def flat(values):
    return values.reshape((-1,) + values.shape[4:])


def forward_dot(fields, links):
    return lax.dot_general(fields, links, (((2,), (2,)), ((0,), (0,))), preferred_element_type=F32)


def backward_dot(fields, links):
    return lax.dot_general(fields, links, (((2,), (1,)), ((0,), (0,))), preferred_element_type=F32)


def whole(mesh_size, value):
    return lax.rem(value + mesh_size, mesh_size)


class Place:
    def __init__(self, sizes, row_len):
        self.sizes = sizes
        self.row_len = row_len
        self.gx = lax.axis_index("gx")
        self.gz = lax.axis_index("gz")
        self.ta = lax.axis_index("ta")

    def at(self, gx=0, gz=0, ta=0, flip_gx=0, flip_ta=0):
        x = whole(self.sizes["gx"], self.gx + gx)
        z = whole(self.sizes["gz"], self.gz + gz)
        t = whole(self.sizes["ta"], self.ta + ta)
        if flip_gx:
            x = x + 1 - 2 * lax.rem(x, 2)
        if flip_ta & 1:
            t = t + 1 - 2 * lax.rem(t, 2)
        if flip_ta & 2:
            t = whole(self.sizes["ta"], t + 2)
        return {"gx": x, "gz": z, "ta": t}

    def ahead(self, direction, sign):
        if direction == 0:
            return self.at(gx=sign * self.row_len)
        if direction == 1:
            return self.at(gx=sign)
        if direction == 2:
            return self.at(gz=sign)
        return self.at(ta=sign)

    def stage(self, index):
        if index == 0:
            return [self.at(flip_ta=1)]
        if index == 1:
            turns = [(a, c, k) for k in (2, 1, 3, 0) for a in (1, 0) for c in (2, 0)]
            return [self.at(gz=k, flip_gx=a, flip_ta=c) for a, c, k in turns[:-1]]
        far = [16] + [sign * k for k in range(15, 0, -1) for sign in (1, -1)]
        return [self.at(gx=2 * k) for k in far]


def twice(values):
    return jnp.concatenate([values, values], axis=-1)


def turned(values):
    return pltpu.roll(values, 64, values.ndim - 1)


def groups():
    return [(x, y, z) for x in range(EXT[0]) for y in range(EXT[1]) for z in range(EXT[2])]


def signs():
    lane = lax.broadcasted_iota(jnp.int32, (1, 1, 128), 2)
    return jnp.where(lax.rem(lane, 64) < 32, 1.0, -1.0).astype(F32), lane < 64


def pack_links(hops, packed, pair):
    for g in groups():
        packed[g + (slice(None), slice(None), slice(128 * pair, 128 * pair + 128))] = jnp.concatenate(
            [hops[(2 * pair,) + g], hops[(2 * pair + 1,) + g]], axis=-1
        )


def local_apply(fields, outs, backs, links, packed, split, ahead_sum):
    chi, lower = signs()
    height = 16 * len(fields)
    rows = slice(0, height)
    for k, field in enumerate(fields):
        top = field[...].astype(BF16).astype(F32)
        split[..., 16 * k : 16 * k + 8, :] = top
        split[..., 16 * k + 8 : 16 * k + 16, :] = field[...] - top
    nil = jnp.zeros((4, height, 128), F32)
    for x, y, z in groups():
        own = split[x, y, z, :, rows, :]
        in_x = split[1, y, z, :, rows, :] if x == 0 else nil
        in_y = split[x, 1, z, :, rows, :] if y == 0 else nil
        in_z = split[x, y, z + 1, :, rows, :] if z < 3 else nil
        in_t = jnp.concatenate([own[1:], nil[:1]], axis=0)
        ahead = jnp.concatenate(
            [jnp.where(lower, in_x, in_y).astype(BF16), jnp.where(lower, in_z, in_t).astype(BF16)], axis=-1
        )
        onward = forward_dot(ahead, packed[x, y, z])
        onward = onward + forward_dot(own[..., :64].astype(BF16), links[x, y, z])
        back = backward_dot((own * chi)[..., :64].astype(BF16), packed[x, y, z])
        for k in range(len(fields)):
            a, b = slice(16 * k, 16 * k + 8), slice(16 * k + 8, 16 * k + 16)
            ahead_sum[x, y, z, :, 8 * k : 8 * k + 8, :] = onward[:, a] + onward[:, b]
            backs[k][x, y, z] = back[:, a] + back[:, b]
    nil = jnp.zeros((4, 8, 128), F32)
    for k, (field, out) in enumerate(zip(fields, outs)):
        for x, y, z in groups():
            first, second = slice(0, 128), slice(128, 256)
            in_x = backs[k][0, y, z, :, :, first] if x else nil
            in_y = backs[k][x, 0, z, :, :, first] if y else nil
            in_z = backs[k][x, y, z - 1, :, :, second] if z else nil
            in_t = jnp.concatenate([nil[:1], backs[k][x, y, z, 0:3, :, second]], axis=0)
            total = chi * (jnp.where(lower, in_x, in_y) + jnp.where(lower, in_z, in_t))
            onward = ahead_sum[x, y, z, :, 8 * k : 8 * k + 8, :]
            total = total + jnp.concatenate([onward, jnp.zeros_like(onward)], axis=-1)
            out[x, y, z] = 4.0 * field[x, y, z] + (total + turned(total))


def on_device(sizes, row_len, rhs_hbm, self_hbm, hop_hbm, sol_ref, res_ref,
              rhs_in, links, hops, packed, split, ahead_sum, back_a, back_b, back_c, back_d, halo_in,
              rhs, m0, m1, r1, d0, z_field, rt, lt, lz, lt2, lz2, d1,
              send_xy, send_zt, got_xy, got_zt, rows_out, rows_in,
              load_sem, halo_send, halo_recv, sum_send, sum_recv):
    place = Place(sizes, row_len)
    loads = [pltpu.make_async_copy(rhs_hbm, rhs_in, load_sem.at[0])]
    for d in range(4):
        loads.append(pltpu.make_async_copy(hop_hbm.at[d], hops.at[d], load_sem.at[1 + d]))
    loads.append(pltpu.make_async_copy(self_hbm, links, load_sem.at[5]))
    for load in loads:
        load.start()

    greeted = [place.ahead(d, sign) for d in range(4) for sign in (1, -1)]
    for index in range(len(STAGES)):
        greeted += place.stage(index)
    barrier = pltpu.get_barrier_semaphore()
    for other in greeted:
        pl.semaphore_signal(barrier, inc=1, device_id=other, device_id_type=MESH)

    chi, lower = signs()
    lane_r = lax.broadcasted_iota(jnp.int32, (8, 128), 1)
    sub_r = lax.broadcasted_iota(jnp.int32, (8, 128), 0)

    def dot_sum(a, b):
        summed = jnp.sum(flat(a[...]) * flat(b[...]), axis=0)
        return jnp.sum(summed[:, :64], axis=-1, keepdims=True)

    def to_row(columns):
        spread = jnp.zeros((8, 128), F32)
        for k, column in enumerate(columns):
            spread = jnp.where(lane_r == 8 * k + sub_r, column, spread)
        return jnp.sum(spread, axis=0, keepdims=True)

    def from_row(row, k):
        return jnp.sum(jnp.where(lane_r == 8 * k + sub_r, row, 0.0), axis=1, keepdims=True)

    def apply(fields, outs, backs):
        local_apply(fields, outs, backs, links, packed, split, ahead_sum)

    def face_ref(store, around, d, kind):
        xy, zt = store
        return (xy if d < 2 else zt).at[around, d % 2, kind]

    def halo_copy(around, d, kind):
        slot = (around * 4 + d) * 2 + kind
        return pltpu.make_async_remote_copy(
            src_ref=face_ref((send_xy, send_zt), around, d, kind),
            dst_ref=face_ref((got_xy, got_zt), around, d, kind),
            send_sem=halo_send.at[slot],
            recv_sem=halo_recv.at[slot],
            device_id=place.ahead(d, -1 if kind == 0 else 1),
            device_id_type=MESH,
        )

    def halo_start(around, field, back_of):
        for d in range(4):
            low = flat(field[part(d, 0, 1)])
            half = low.shape[0] // 2
            face_ref((send_xy, send_zt), around, d, 0)[...] = jnp.where(lower, low[:half], low[half:]).astype(BF16)
            halo_copy(around, d, 0).start()
            lanes = slice(128 * (d // 2), 128 * (d // 2) + 128)
            back = flat(chi * back_of(part(d, EXT[d] - 1, EXT[d]) + (slice(None), lanes)))
            if d % 2:
                back = jnp.where(lower, turned(back[:half]), back[half:])
            else:
                back = jnp.where(lower, back[:half], turned(back[half:]))
            face_ref((send_xy, send_zt), around, d, 1)[...] = back.astype(BF16)
            halo_copy(around, d, 1).start()

    def halo_finish(around, out):
        for d in (2, 3, 1, 0):
            shape = tuple(1 if k == d else EXT[k] for k in range(4)) + (8, 128)
            halo_copy(around, d, 0).wait_recv()
            got = face_ref((got_xy, got_zt), around, d, 0)[...].astype(F32)
            pieces = (turned(got), got) if d % 2 else (got, turned(got))
            lanes = slice(64 * (d % 2), 64 * (d % 2) + 64)
            place_in = slice(64 * d, 64 * d + 64)
            field = jnp.concatenate(pieces, axis=0).reshape(shape)[..., lanes]
            halo_in[part(d, EXT[d] - 1, EXT[d]) + (slice(None), place_in)] = field
            halo_copy(around, d, 1).wait_recv()
            got = face_ref((got_xy, got_zt), around, d, 1)[...].astype(F32)
            other = turned(got)
            both = jnp.concatenate([jnp.where(lower, got, other), jnp.where(lower, other, got)], axis=0)
            out[part(d, 0, 1)] += both.reshape(shape)
        for g in groups():
            onward = forward_dot(halo_in[g].astype(BF16), packed[g])
            out[g] += twice(onward)

    def sum_copies(around, index):
        base = around * SLOTS + sum(STAGES[:index])
        return [
            pltpu.make_async_remote_copy(
                src_ref=rows_out.at[around * 4 + index],
                dst_ref=rows_in.at[base + k],
                send_sem=sum_send.at[base + k],
                recv_sem=sum_recv.at[base + k],
                device_id=other,
                device_id_type=MESH,
            )
            for k, other in enumerate(place.stage(index))
        ]

    def mesh_sum(around, row, meanwhile=None):
        for index in range(len(STAGES)):
            base = around * SLOTS + sum(STAGES[:index])
            rows_out[around * 4 + index] = row
            copies = sum_copies(around, index)
            for copy in copies:
                copy.start()
            if index == len(STAGES) - 1 and meanwhile is not None:
                meanwhile()
            for copy in copies:
                copy.wait_recv()
            row = row + jnp.sum(rows_in[base : base + len(copies)], axis=0)
        return row

    halo_in[...] = jnp.zeros_like(halo_in)
    loads[0].wait()
    rhs[...] = twice(rhs_in[...])
    for pair in range(2):
        loads[1 + 2 * pair].wait()
        loads[2 + 2 * pair].wait()
        pack_links(hops, packed, pair)
    loads[5].wait()
    apply([rhs], [m0], [back_a])
    weight_a = dot_sum(m0, rhs) / dot_sum(m0, m0)
    r1[...] = rhs[...] - weight_a * m0[...]
    apply([r1], [m1], [back_b])
    weight_b = dot_sum(m1, r1) / dot_sum(m1, m1)
    d0[...] = weight_a * rhs[...] + weight_b * r1[...]
    pl.semaphore_wait(barrier, len(greeted))
    halo_start(0, d0, lambda at: weight_a * back_a[at] + weight_b * back_b[at])
    z_field[...] = weight_a * m0[...] + weight_b * m1[...]
    halo_finish(0, z_field)

    part_zr, part_zz = dot_sum(z_field, rhs), dot_sum(z_field, z_field)
    centre = jnp.where(part_zz > 0.0, part_zr / jnp.where(part_zz > 0.0, part_zz, 1.0), 0.0)

    def meanwhile():
        rt[...] = rhs[...] - centre * z_field[...]
        apply([rt, z_field], [lt, lz], [back_a, back_b])
        apply([lt, lz], [lt2, lz2], [back_c, back_d])

    sums = mesh_sum(0, to_row([part_zr, part_zz]), meanwhile)
    sum_zz = from_row(sums, 1)
    alpha = from_row(sums, 0) / sum_zz
    shift = alpha - centre
    r1[...] = rhs[...] - alpha * z_field[...]
    m0[...] = lt[...] - shift * lz[...]
    weight_a = dot_sum(m0, r1) / dot_sum(m0, m0)
    m1[...] = m0[...] - weight_a * (lt2[...] - shift * lz2[...])
    rt[...] = r1[...] - weight_a * m0[...]
    weight_b = dot_sum(m1, rt) / dot_sum(m1, m1)
    d1[...] = weight_a * r1[...] + weight_b * rt[...]
    near = weight_a + weight_b
    deep = weight_a * weight_b

    def back_of(at):
        return near * (back_a[at] - shift * back_b[at]) - deep * (back_c[at] - shift * back_d[at])

    halo_start(1, d1, back_of)
    lz[...] = weight_a * m0[...] + weight_b * m1[...]
    halo_finish(1, lz)

    columns = [dot_sum(z_field, lz), dot_sum(lz, r1), dot_sum(lz, lz), dot_sum(z_field, r1)]
    sums = mesh_sum(1, to_row(columns))
    cross, onto, square, kept = [from_row(sums, k) for k in range(4)]
    beta = cross / sum_zz
    alpha_b = (onto - beta * kept) / (square - beta * (2.0 * cross - beta * sum_zz))
    sol_ref[...] = (alpha * d0[...] + alpha_b * (d1[...] - beta * d0[...]))[..., :64]
    res_ref[...] = (r1[...] - alpha_b * (lz[...] - beta * z_field[...]))[..., :64]

    for around in range(2):
        for d in range(4):
            for kind in range(2):
                halo_copy(around, d, kind).wait_send()
        for index in range(len(STAGES)):
            for copy in sum_copies(around, index):
                copy.wait_send()


def solution(mesh):
    sizes = dict(mesh.shape)
    row_len = min(8, max(2, sizes["gx"] // 8))

    def step(rhs, self_coupling, hopping):
        field = EXT + (8, 64)
        vmem = pl.BlockSpec(memory_space=pltpu.VMEM)
        hbm = pl.BlockSpec(memory_space=pl.ANY)
        fields = [pltpu.VMEM(EXT + (8, 128), F32)] * 12
        backs = [pltpu.VMEM(EXT + (8, 256), F32)] * 5
        sol, res = pl.pallas_call(
            functools.partial(on_device, sizes, row_len),
            out_shape=[jax.ShapeDtypeStruct(field, F32)] * 2,
            in_specs=[hbm] * 3,
            out_specs=[vmem] * 2,
            scratch_shapes=[
                pltpu.VMEM(field, F32),
                pltpu.VMEM(EXT + (64, 64), BF16),
                pltpu.VMEM((4,) + EXT + (64, 64), BF16),
                pltpu.VMEM(EXT + (64, 256), BF16),
                pltpu.VMEM(EXT + (32, 128), F32),
                pltpu.VMEM(EXT + (16, 64), F32),
                *backs,
                *fields,
                pltpu.VMEM((2, 2, 2, 16, 8, 128), BF16),
                pltpu.VMEM((2, 2, 2, 8, 8, 128), BF16),
                pltpu.VMEM((2, 2, 2, 16, 8, 128), BF16),
                pltpu.VMEM((2, 2, 2, 8, 8, 128), BF16),
                pltpu.VMEM((8, 1, 128), F32),
                pltpu.VMEM((2 * SLOTS, 1, 128), F32),
                pltpu.SemaphoreType.DMA((6,)),
                pltpu.SemaphoreType.DMA((16,)),
                pltpu.SemaphoreType.DMA((16,)),
                pltpu.SemaphoreType.DMA((2 * SLOTS,)),
                pltpu.SemaphoreType.DMA((2 * SLOTS,)),
            ],
            compiler_params=pltpu.CompilerParams(collective_id=0, has_side_effects=True),
        )(rhs[0], self_coupling[0], hopping[:, 0])
        return sol[None], res[None]

    whole_spec = P("gx", None, None, "gz", "ta", None, None)
    return jax.shard_map(
        step,
        mesh=mesh,
        in_specs=(whole_spec, whole_spec, P(None, "gx", None, None, "gz", "ta", None, None)),
        out_specs=(whole_spec, whole_spec),
        check_vma=False,
    )
```

time: 90.9 us -> 85.1 us (0.936); the launches traced: 89.5 us -> 84.9 us
  Pallas kernels: 85.5 us -> 80.9 us
    pallas_call x1, Pallas kernels: 85.5 us -> 80.9 us  [step(): pl.pallas_call(functools.partial(on_device, sizes, row_len), out_shape=[j...]
where the time goes in v2:
time: 85.1 us; the launch traced here: 84.9 us
  Pallas kernels  80.9 us (95%)
  local copies, waits for them, and re-layouts  3.34 us (4%)
    pallas_call x1, Pallas kernels, step(): pl.pallas_call(functools.partial(on_device, sizes, row_len), out_shape=[j...  80.9 us
    unnamed x2, local copies, waits for them, and re-layouts  3.34 us

profile of v2, /device:TPU:1, one launch (start us, length us, event | category | flops | bytes accessed | tf_op | source)
XLA Modules:
  0.0 84.9 jit_solution(10056704202967587426)
XLA Ops:
  0.6 80.9 %shard_map.50 = (f32[2,2,4,4,8,64]{5,4,3,2,1,0:T(8,128)}, f32[2,2,4,4,8,64]{5,4,3,2,1,0:T(8,128)}) custom-call(f32[2,2,4,4,8,64]{5,4,3,2,1,0:T(8,128)} %bitcast.9, bf16[2,2,4,4,64,64]{5,4,3,2,1,0:T(8,128)(2,1)} %bitcast.6, bf16[4,2,2,4,4,64,64]{6,5,4,3,2,1,0:T(8,128)(2,1)} %bitcast.5), custom_call_target="tpu_custom_call" | custom-call | tf_op jit(solution)/shard_map/pallas_call | solution.py:332
  81.5 1.7 %copy.7 = f32[1,2,2,4,4,8,64]{6,5,4,3,2,1,0:T(8,128)} copy(f32[1,2,2,4,4,8,64]{6,5,4,3,2,1,0:T(8,128)} %bitcast.8) | data formatting | bytes 262144
  83.2 1.7 %copy.8 = f32[1,2,2,4,4,8,64]{6,5,4,3,2,1,0:T(8,128)} copy(f32[1,2,2,4,4,8,64]{6,5,4,3,2,1,0:T(8,128)} %bitcast.7) | data formatting | bytes 262144

commit v3 on v2

--- a/solution.py
+++ b/solution.py
@@ -137,11 +137,11 @@
             out[x, y, z] = 4.0 * field[x, y, z] + (total + turned(total))
 
 
-def on_device(sizes, row_len, rhs_hbm, self_hbm, hop_hbm, sol_ref, res_ref,
+def on_device(sizes, row_len, rhs_hbm, self_hbm, hop_hbm, pair_out, zero_out, left_out, scale_out,
               rhs_in, links, hops, packed, split, ahead_sum, back_a, back_b, back_c, back_d, halo_in,
-              rhs, m0, m1, r1, d0, z_field, rt, lt, lz, lt2, lz2, d1,
-              send_xy, send_zt, got_xy, got_zt, rows_out, rows_in,
-              load_sem, halo_send, halo_recv, sum_send, sum_recv):
+              rhs, m0, n0, m1, r1, d0, z_field, rt, lt, lz, lt2, lz2, d1, raw, left,
+              send_xy, send_zt, got_xy, got_zt, rows_out, rows_in, gram_out, gram_in,
+              load_sem, halo_send, halo_recv, sum_send, sum_recv, gram_send, gram_recv):
     place = Place(sizes, row_len)
     loads = [pltpu.make_async_copy(rhs_hbm, rhs_in, load_sem.at[0])]
     for d in range(4):
@@ -192,14 +192,18 @@
             device_id_type=MESH,
         )
 
-    def halo_start(around, field, back_of):
+    def send_fields(around, field):
         for d in range(4):
             low = flat(field[part(d, 0, 1)])
             half = low.shape[0] // 2
             face_ref((send_xy, send_zt), around, d, 0)[...] = jnp.where(lower, low[:half], low[half:]).astype(BF16)
             halo_copy(around, d, 0).start()
+
+    def send_backs(around, back_of):
+        for d in range(4):
             lanes = slice(128 * (d // 2), 128 * (d // 2) + 128)
             back = flat(chi * back_of(part(d, EXT[d] - 1, EXT[d]) + (slice(None), lanes)))
+            half = back.shape[0] // 2
             if d % 2:
                 back = jnp.where(lower, turned(back[:half]), back[half:])
             else:
@@ -207,24 +211,50 @@
             face_ref((send_xy, send_zt), around, d, 1)[...] = back.astype(BF16)
             halo_copy(around, d, 1).start()
 
-    def halo_finish(around, out):
+    def received(around, d, kind):
+        halo_copy(around, d, kind).wait_recv()
+        return face_ref((got_xy, got_zt), around, d, kind)[...].astype(F32)
+
+    def halo_finish(out, face):
         for d in (2, 3, 1, 0):
             shape = tuple(1 if k == d else EXT[k] for k in range(4)) + (8, 128)
-            halo_copy(around, d, 0).wait_recv()
-            got = face_ref((got_xy, got_zt), around, d, 0)[...].astype(F32)
+            got = face(d, 0)
             pieces = (turned(got), got) if d % 2 else (got, turned(got))
             lanes = slice(64 * (d % 2), 64 * (d % 2) + 64)
             place_in = slice(64 * d, 64 * d + 64)
             field = jnp.concatenate(pieces, axis=0).reshape(shape)[..., lanes]
             halo_in[part(d, EXT[d] - 1, EXT[d]) + (slice(None), place_in)] = field
-            halo_copy(around, d, 1).wait_recv()
-            got = face_ref((got_xy, got_zt), around, d, 1)[...].astype(F32)
+            got = face(d, 1)
             other = turned(got)
             both = jnp.concatenate([jnp.where(lower, got, other), jnp.where(lower, other, got)], axis=0)
             out[part(d, 0, 1)] += both.reshape(shape)
         for g in groups():
             onward = forward_dot(halo_in[g].astype(BF16), packed[g])
             out[g] += twice(onward)
+
+    def gram_copies():
+        return [
+            pltpu.make_async_remote_copy(
+                src_ref=gram_out.at[0],
+                dst_ref=gram_in.at[2 * d + kind],
+                send_sem=gram_send.at[2 * d + kind],
+                recv_sem=gram_recv.at[2 * d + kind],
+                device_id=place.ahead(d, -1 if kind == 0 else 1),
+                device_id_type=MESH,
+            )
+            for d in range(4)
+            for kind in range(2)
+        ]
+
+    def neighbour_weights(columns, alpha):
+        shift = alpha - columns[0]
+        onto, square, deep_onto, deep_cross, deep_square = [
+            columns[k] - shift * (columns[k + 1] - shift * columns[k + 2]) for k in (1, 4, 7, 10, 13)
+        ]
+        first = onto / square
+        top = onto - first * square - first * (deep_onto - first * deep_cross)
+        second = top / (square - first * (2.0 * deep_cross - first * deep_square))
+        return first + second, first * second
 
     def sum_copies(around, index):
         base = around * SLOTS + sum(STAGES[:index])
@@ -240,15 +270,15 @@
             for k, other in enumerate(place.stage(index))
         ]
 
-    def mesh_sum(around, row, meanwhile=None):
+    def mesh_sum(around, row, meanwhile=(None, None, None)):
         for index in range(len(STAGES)):
             base = around * SLOTS + sum(STAGES[:index])
             rows_out[around * 4 + index] = row
             copies = sum_copies(around, index)
             for copy in copies:
                 copy.start()
-            if index == len(STAGES) - 1 and meanwhile is not None:
-                meanwhile()
+            if meanwhile[index] is not None:
+                meanwhile[index]()
             for copy in copies:
                 copy.wait_recv()
             row = row + jnp.sum(rows_in[base : base + len(copies)], axis=0)
@@ -263,60 +293,126 @@
         pack_links(hops, packed, pair)
     loads[5].wait()
     apply([rhs], [m0], [back_a])
+    apply([m0], [n0], [back_b])
     weight_a = dot_sum(m0, rhs) / dot_sum(m0, m0)
     r1[...] = rhs[...] - weight_a * m0[...]
-    apply([r1], [m1], [back_b])
+    m1[...] = m0[...] - weight_a * n0[...]
     weight_b = dot_sum(m1, r1) / dot_sum(m1, m1)
+    near, deep = weight_a + weight_b, weight_a * weight_b
     d0[...] = weight_a * rhs[...] + weight_b * r1[...]
     pl.semaphore_wait(barrier, len(greeted))
-    halo_start(0, d0, lambda at: weight_a * back_a[at] + weight_b * back_b[at])
+    send_fields(0, d0)
+    send_backs(0, lambda at: near * back_a[at] - deep * back_b[at])
+    send_fields(1, rhs)
+    send_backs(1, lambda at: back_a[at])
+    send_fields(2, m0)
+    send_backs(2, lambda at: back_b[at])
     z_field[...] = weight_a * m0[...] + weight_b * m1[...]
-    halo_finish(0, z_field)
+    halo_finish(z_field, lambda d, kind: received(0, d, kind))
 
     part_zr, part_zz = dot_sum(z_field, rhs), dot_sum(z_field, z_field)
-    centre = jnp.where(part_zz > 0.0, part_zr / jnp.where(part_zz > 0.0, part_zz, 1.0), 0.0)
-
-    def meanwhile():
+    columns_in = []
+
+    def in_core_stage():
+        send_fields(3, z_field)
+
+    def in_plane_stage():
+        apply([z_field], [lz], [back_c])
+        send_backs(3, lambda at: back_c[at])
+        send_fields(4, lz)
+        apply([lz], [lz2], [back_d])
+        send_backs(4, lambda at: back_d[at])
+
+    def in_column_stage():
+        centre = jnp.where(part_zz > 0.0, part_zr / jnp.where(part_zz > 0.0, part_zz, 1.0), 0.0)
         rt[...] = rhs[...] - centre * z_field[...]
-        apply([rt, z_field], [lt, lz], [back_a, back_b])
-        apply([lt, lz], [lt2, lz2], [back_c, back_d])
-
-    sums = mesh_sum(0, to_row([part_zr, part_zz]), meanwhile)
+        lt[...] = m0[...] - centre * lz[...]
+        lt2[...] = n0[...] - centre * lz2[...]
+        gram = [
+            centre,
+            dot_sum(lt, rt), dot_sum(lt, z_field) + dot_sum(lz, rt), dot_sum(lz, z_field),
+            dot_sum(lt, lt), 2.0 * dot_sum(lt, lz), dot_sum(lz, lz),
+            dot_sum(lt2, rt), dot_sum(lt2, z_field) + dot_sum(lz2, rt), dot_sum(lz2, z_field),
+            dot_sum(lt2, lt), dot_sum(lt2, lz) + dot_sum(lz2, lt), dot_sum(lz2, lz),
+            dot_sum(lt2, lt2), 2.0 * dot_sum(lt2, lz2), dot_sum(lz2, lz2),
+        ]
+        gram_out[0] = to_row(gram)
+        copies = gram_copies()
+        for copy in copies:
+            copy.start()
+        near, deep = neighbour_weights(gram, centre)
+        d1[...] = near * rt[...] - deep * lt[...]
+        send_fields(5, d1)
+        send_backs(
+            5,
+            lambda at: near * (back_a[at] - centre * back_c[at]) - deep * (back_b[at] - centre * back_d[at]),
+        )
+        for k, copy in enumerate(copies):
+            copy.wait_recv()
+            row = gram_in[k]
+            columns = [from_row(row, c) for c in range(16)]
+            columns_in.append((columns, neighbour_weights(columns, columns[0])))
+
+    sums = mesh_sum(0, to_row([part_zr, part_zz]), (in_core_stage, in_plane_stage, in_column_stage))
     sum_zz = from_row(sums, 1)
     alpha = from_row(sums, 0) / sum_zz
-    shift = alpha - centre
     r1[...] = rhs[...] - alpha * z_field[...]
-    m0[...] = lt[...] - shift * lz[...]
-    weight_a = dot_sum(m0, r1) / dot_sum(m0, m0)
-    m1[...] = m0[...] - weight_a * (lt2[...] - shift * lz2[...])
-    rt[...] = r1[...] - weight_a * m0[...]
-    weight_b = dot_sum(m1, rt) / dot_sum(m1, m1)
-    d1[...] = weight_a * r1[...] + weight_b * rt[...]
-    near = weight_a + weight_b
-    deep = weight_a * weight_b
-
-    def back_of(at):
-        return near * (back_a[at] - shift * back_b[at]) - deep * (back_c[at] - shift * back_d[at])
-
-    halo_start(1, d1, back_of)
-    lz[...] = weight_a * m0[...] + weight_b * m1[...]
-    halo_finish(1, lz)
-
-    columns = [dot_sum(z_field, lz), dot_sum(lz, r1), dot_sum(lz, lz), dot_sum(z_field, r1)]
-    sums = mesh_sum(1, to_row(columns))
+    lt[...] = m0[...] - alpha * lz[...]
+    weight_a = dot_sum(lt, r1) / dot_sum(lt, lt)
+    m1[...] = lt[...] - weight_a * (n0[...] - alpha * lz2[...])
+    left[...] = r1[...] - weight_a * lt[...]
+    weight_b = dot_sum(m1, left) / dot_sum(m1, m1)
+    d1[...] = weight_a * r1[...] + weight_b * left[...]
+    raw[...] = weight_a * lt[...] + weight_b * m1[...]
+
+    def face(d, kind):
+        columns, (near_mid, deep_mid) = columns_in[2 * d + kind]
+        near, deep = neighbour_weights(columns, alpha)
+        source, mapped, zero, again, middle = [received(around, d, kind) for around in range(1, 6)]
+        centre, shift = columns[0], alpha - columns[0]
+        more, less = near - near_mid, deep - deep_mid
+        return (middle + more * source - less * mapped - (more * centre + near * shift) * zero
+                + (less * centre + deep * shift) * again)
+
+    halo_finish(raw, face)
+
+    columns = [dot_sum(z_field, raw), dot_sum(raw, r1), dot_sum(raw, raw), dot_sum(z_field, r1)]
+    outs = [pltpu.make_async_copy(source, place_out, load_sem.at[k])
+            for k, (source, place_out) in enumerate(((rt, pair_out), (lt2, zero_out), (r1, left_out)))]
+
+    def in_last_stage():
+        rt[...] = jnp.where(lower, d0[...], d1[...])
+        lt2[...] = jnp.where(lower, z_field[...], raw[...])
+        for out in outs:
+            out.start()
+
+    sums = mesh_sum(1, to_row(columns), (None, None, in_last_stage))
     cross, onto, square, kept = [from_row(sums, k) for k in range(4)]
     beta = cross / sum_zz
     alpha_b = (onto - beta * kept) / (square - beta * (2.0 * cross - beta * sum_zz))
-    sol_ref[...] = (alpha * d0[...] + alpha_b * (d1[...] - beta * d0[...]))[..., :64]
-    res_ref[...] = (r1[...] - alpha_b * (lz[...] - beta * z_field[...]))[..., :64]
-
-    for around in range(2):
+    half = lane_r < 64
+    scale_out[0] = jnp.where(half, alpha - alpha_b * beta, alpha_b)
+    scale_out[1] = jnp.where(half, alpha_b * beta, -alpha_b)
+
+    for out in outs:
+        out.wait()
+    for around in range(6):
         for d in range(4):
             for kind in range(2):
                 halo_copy(around, d, kind).wait_send()
+    for copy in gram_copies():
+        copy.wait_send()
+    for around in range(2):
         for index in range(len(STAGES)):
             for copy in sum_copies(around, index):
                 copy.wait_send()
+
+
+def combine(pair_ref, zero_ref, left_ref, scale_ref, sol_ref, res_ref):
+    first = scale_ref[0] * pair_ref[...]
+    second = scale_ref[1] * zero_ref[...]
+    sol_ref[...] = (first + turned(first))[..., :64]
+    res_ref[...] = (left_ref[...] + (second + turned(second)))[..., :64]
 
 
 def solution(mesh):
@@ -327,36 +423,46 @@
         field = EXT + (8, 64)
         vmem = pl.BlockSpec(memory_space=pltpu.VMEM)
         hbm = pl.BlockSpec(memory_space=pl.ANY)
-        fields = [pltpu.VMEM(EXT + (8, 128), F32)] * 12
+        fields = [pltpu.VMEM(EXT + (8, 128), F32)] * 15
         backs = [pltpu.VMEM(EXT + (8, 256), F32)] * 5
-        sol, res = pl.pallas_call(
+        parts = pl.pallas_call(
             functools.partial(on_device, sizes, row_len),
-            out_shape=[jax.ShapeDtypeStruct(field, F32)] * 2,
+            out_shape=[jax.ShapeDtypeStruct(EXT + (8, 128), F32)] * 3 + [jax.ShapeDtypeStruct((2, 8, 128), F32)],
             in_specs=[hbm] * 3,
-            out_specs=[vmem] * 2,
+            out_specs=[hbm] * 3 + [vmem],
             scratch_shapes=[
                 pltpu.VMEM(field, F32),
                 pltpu.VMEM(EXT + (64, 64), BF16),
                 pltpu.VMEM((4,) + EXT + (64, 64), BF16),
                 pltpu.VMEM(EXT + (64, 256), BF16),
-                pltpu.VMEM(EXT + (32, 128), F32),
-                pltpu.VMEM(EXT + (16, 64), F32),
+                pltpu.VMEM(EXT + (16, 128), F32),
+                pltpu.VMEM(EXT + (8, 64), F32),
                 *backs,
                 *fields,
-                pltpu.VMEM((2, 2, 2, 16, 8, 128), BF16),
-                pltpu.VMEM((2, 2, 2, 8, 8, 128), BF16),
-                pltpu.VMEM((2, 2, 2, 16, 8, 128), BF16),
-                pltpu.VMEM((2, 2, 2, 8, 8, 128), BF16),
+                pltpu.VMEM((6, 2, 2, 16, 8, 128), BF16),
+                pltpu.VMEM((6, 2, 2, 8, 8, 128), BF16),
+                pltpu.VMEM((6, 2, 2, 16, 8, 128), BF16),
+                pltpu.VMEM((6, 2, 2, 8, 8, 128), BF16),
                 pltpu.VMEM((8, 1, 128), F32),
                 pltpu.VMEM((2 * SLOTS, 1, 128), F32),
+                pltpu.VMEM((1, 1, 128), F32),
+                pltpu.VMEM((8, 1, 128), F32),
                 pltpu.SemaphoreType.DMA((6,)),
-                pltpu.SemaphoreType.DMA((16,)),
-                pltpu.SemaphoreType.DMA((16,)),
+                pltpu.SemaphoreType.DMA((48,)),
+                pltpu.SemaphoreType.DMA((48,)),
                 pltpu.SemaphoreType.DMA((2 * SLOTS,)),
                 pltpu.SemaphoreType.DMA((2 * SLOTS,)),
+                pltpu.SemaphoreType.DMA((8,)),
+                pltpu.SemaphoreType.DMA((8,)),
             ],
             compiler_params=pltpu.CompilerParams(collective_id=0, has_side_effects=True),
         )(rhs[0], self_coupling[0], hopping[:, 0])
+        sol, res = pl.pallas_call(
+            combine,
+            out_shape=[jax.ShapeDtypeStruct(field, F32)] * 2,
+            in_specs=[vmem] * 4,
+            out_specs=[vmem] * 2,
+        )(*parts)
         return sol[None], res[None]
 
     whole_spec = P("gx", None, None, "gz", "ta", None, None)

time: 85.1 us -> 87.6 us (1.029)
  Pallas kernels: 80.9 us -> 86.5 us
  local copies, waits for them, and re-layouts: 3.34 us -> 0 us
    pallas_call x1, Pallas kernels: 80.9 us -> 84.5 us  [step(): pl.pallas_call(functools.partial(on_device, sizes, row_len), out_shape=[j...]
    unnamed x2 -> x0, local copies, waits for them, and re-layouts: 3.34 us -> none
    pallas_call x0 -> x1, Pallas kernels: none -> 2.04 us  [step(): pl.pallas_call(combine, out_shape=[jax.ShapeDtypeStruct(field, F32)] * 2,...]
where the time goes in v3:
time: 87.6 us; the launch traced here: 87.2 us
  Pallas kernels  86.5 us (99%)
    pallas_call x1, Pallas kernels, step(): pl.pallas_call(functools.partial(on_device, sizes, row_len), out_shape=[j...  84.5 us
    pallas_call x1, Pallas kernels, step(): pl.pallas_call(combine, out_shape=[jax.ShapeDtypeStruct(field, F32)] * 2,...  2.04 us

profile of v3, /device:TPU:1, one launch (start us, length us, event | category | flops | bytes accessed | tf_op | source)
XLA Modules:
  0.0 87.2 jit_solution(17101559038840128815)
XLA Ops:
  0.6 84.5 %shard_map.50 = (f32[2,2,4,4,8,128]{5,4,3,2,1,0:T(8,128)}, f32[2,2,4,4,8,128]{5,4,3,2,1,0:T(8,128)}, f32[2,2,4,4,8,128]{5,4,3,2,1,0:T(8,128)}, f32[2,8,128]{2,1,0:T(8,128)}) custom-call(f32[2,2,4,4,8,64]{5,4,3,2,1,0:T(8,128)} %bitcast.7, bf16[2,2,4,4,64,64]{5,4,3,2,1,0:T(8,128)(2,1)} %bitcast.6, bf16[4,2,2,4,4,64,64]{6,5,4,3,2,1,0:T(8,128)(2,1)} %bitcast.5), custom_call_target="tpu_custom_call" | custom-call | tf_op jit(solution)/shard_map/pallas_call | solution.py:428
  85.1 2.0 %shard_map.51 = (f32[2,2,4,4,8,64]{5,4,3,2,1,0:T(8,128)}, f32[2,2,4,4,8,64]{5,4,3,2,1,0:T(8,128)}) custom-call(f32[2,2,4,4,8,128]{5,4,3,2,1,0:T(8,128)} %get-tuple-element.8.pair_ref, f32[2,2,4,4,8,128]{5,4,3,2,1,0:T(8,128)} %get-tuple-element.9.zero_ref, f32[2,2,4,4,8,128]{5,4,3,2,1,0:T(8,128)} %get-tuple-element.10.left_ref, ...), custom_call_target="tpu_custom_call" | custom-call | tf_op jit(solution)/shard_map/pallas_call | solution.py:460

commit v4 on v3

--- a/solution.py
+++ b/solution.py
@@ -11,7 +11,7 @@
 EXT = (2, 2, 4, 4)
 F32 = jnp.float32
 BF16 = jnp.bfloat16
-STAGES = (1, 15, 31)
+STAGES = (15, 63)
 SLOTS = sum(STAGES)
 
 
@@ -66,12 +66,10 @@
 
     def stage(self, index):
         if index == 0:
-            return [self.at(flip_ta=1)]
-        if index == 1:
             turns = [(a, c, k) for k in (2, 1, 3, 0) for a in (1, 0) for c in (2, 0)]
             return [self.at(gz=k, flip_gx=a, flip_ta=c) for a, c, k in turns[:-1]]
         far = [16] + [sign * k for k in range(15, 0, -1) for sign in (1, -1)]
-        return [self.at(gx=2 * k) for k in far]
+        return [self.at(gx=2 * k, flip_ta=c) for k in far for c in (0, 1)] + [self.at(flip_ta=1)]
 
 
 def twice(values):
@@ -139,9 +137,9 @@
 
 def on_device(sizes, row_len, rhs_hbm, self_hbm, hop_hbm, pair_out, zero_out, left_out, scale_out,
               rhs_in, links, hops, packed, split, ahead_sum, back_a, back_b, back_c, back_d, halo_in,
-              rhs, m0, n0, m1, r1, d0, z_field, rt, lt, lz, lt2, lz2, d1, raw, left,
-              send_xy, send_zt, got_xy, got_zt, rows_out, rows_in, gram_out, gram_in,
-              load_sem, halo_send, halo_recv, sum_send, sum_recv, gram_send, gram_recv):
+              rhs, m0, n0, m1, r1, d0, z_field, rt, lt, lz, lt2, lz2, d1, raw,
+              send_xy, send_zt, got_xy, got_zt, rows_out, rows_in,
+              load_sem, halo_send, halo_recv, sum_send, sum_recv):
     place = Place(sizes, row_len)
     loads = [pltpu.make_async_copy(rhs_hbm, rhs_in, load_sem.at[0])]
     for d in range(4):
@@ -232,21 +230,7 @@
             onward = forward_dot(halo_in[g].astype(BF16), packed[g])
             out[g] += twice(onward)
 
-    def gram_copies():
-        return [
-            pltpu.make_async_remote_copy(
-                src_ref=gram_out.at[0],
-                dst_ref=gram_in.at[2 * d + kind],
-                send_sem=gram_send.at[2 * d + kind],
-                recv_sem=gram_recv.at[2 * d + kind],
-                device_id=place.ahead(d, -1 if kind == 0 else 1),
-                device_id_type=MESH,
-            )
-            for d in range(4)
-            for kind in range(2)
-        ]
-
-    def neighbour_weights(columns, alpha):
+    def smoothing_weights(columns, alpha):
         shift = alpha - columns[0]
         onto, square, deep_onto, deep_cross, deep_square = [
             columns[k] - shift * (columns[k + 1] - shift * columns[k + 2]) for k in (1, 4, 7, 10, 13)
@@ -270,7 +254,7 @@
             for k, other in enumerate(place.stage(index))
         ]
 
-    def mesh_sum(around, row, meanwhile=(None, None, None)):
+    def mesh_sum(around, row, meanwhile=(None, None)):
         for index in range(len(STAGES)):
             base = around * SLOTS + sum(STAGES[:index])
             rows_out[around * 4 + index] = row
@@ -303,78 +287,39 @@
     pl.semaphore_wait(barrier, len(greeted))
     send_fields(0, d0)
     send_backs(0, lambda at: near * back_a[at] - deep * back_b[at])
-    send_fields(1, rhs)
-    send_backs(1, lambda at: back_a[at])
-    send_fields(2, m0)
-    send_backs(2, lambda at: back_b[at])
     z_field[...] = weight_a * m0[...] + weight_b * m1[...]
     halo_finish(z_field, lambda d, kind: received(0, d, kind))
 
     part_zr, part_zz = dot_sum(z_field, rhs), dot_sum(z_field, z_field)
-    columns_in = []
-
-    def in_core_stage():
-        send_fields(3, z_field)
-
-    def in_plane_stage():
+    gram = []
+
+    def in_column_stage():
         apply([z_field], [lz], [back_c])
-        send_backs(3, lambda at: back_c[at])
-        send_fields(4, lz)
         apply([lz], [lz2], [back_d])
-        send_backs(4, lambda at: back_d[at])
-
-    def in_column_stage():
         centre = jnp.where(part_zz > 0.0, part_zr / jnp.where(part_zz > 0.0, part_zz, 1.0), 0.0)
         rt[...] = rhs[...] - centre * z_field[...]
         lt[...] = m0[...] - centre * lz[...]
         lt2[...] = n0[...] - centre * lz2[...]
-        gram = [
+        gram.extend([
             centre,
             dot_sum(lt, rt), dot_sum(lt, z_field) + dot_sum(lz, rt), dot_sum(lz, z_field),
             dot_sum(lt, lt), 2.0 * dot_sum(lt, lz), dot_sum(lz, lz),
             dot_sum(lt2, rt), dot_sum(lt2, z_field) + dot_sum(lz2, rt), dot_sum(lz2, z_field),
             dot_sum(lt2, lt), dot_sum(lt2, lz) + dot_sum(lz2, lt), dot_sum(lz2, lz),
             dot_sum(lt2, lt2), 2.0 * dot_sum(lt2, lz2), dot_sum(lz2, lz2),
-        ]
-        gram_out[0] = to_row(gram)
-        copies = gram_copies()
-        for copy in copies:
-            copy.start()
-        near, deep = neighbour_weights(gram, centre)
-        d1[...] = near * rt[...] - deep * lt[...]
-        send_fields(5, d1)
-        send_backs(
-            5,
-            lambda at: near * (back_a[at] - centre * back_c[at]) - deep * (back_b[at] - centre * back_d[at]),
-        )
-        for k, copy in enumerate(copies):
-            copy.wait_recv()
-            row = gram_in[k]
-            columns = [from_row(row, c) for c in range(16)]
-            columns_in.append((columns, neighbour_weights(columns, columns[0])))
-
-    sums = mesh_sum(0, to_row([part_zr, part_zz]), (in_core_stage, in_plane_stage, in_column_stage))
+        ])
+
+    sums = mesh_sum(0, to_row([part_zr, part_zz]), (None, in_column_stage))
     sum_zz = from_row(sums, 1)
     alpha = from_row(sums, 0) / sum_zz
+    near, deep = smoothing_weights(gram, alpha)
     r1[...] = rhs[...] - alpha * z_field[...]
     lt[...] = m0[...] - alpha * lz[...]
-    weight_a = dot_sum(lt, r1) / dot_sum(lt, lt)
-    m1[...] = lt[...] - weight_a * (n0[...] - alpha * lz2[...])
-    left[...] = r1[...] - weight_a * lt[...]
-    weight_b = dot_sum(m1, left) / dot_sum(m1, m1)
-    d1[...] = weight_a * r1[...] + weight_b * left[...]
-    raw[...] = weight_a * lt[...] + weight_b * m1[...]
-
-    def face(d, kind):
-        columns, (near_mid, deep_mid) = columns_in[2 * d + kind]
-        near, deep = neighbour_weights(columns, alpha)
-        source, mapped, zero, again, middle = [received(around, d, kind) for around in range(1, 6)]
-        centre, shift = columns[0], alpha - columns[0]
-        more, less = near - near_mid, deep - deep_mid
-        return (middle + more * source - less * mapped - (more * centre + near * shift) * zero
-                + (less * centre + deep * shift) * again)
-
-    halo_finish(raw, face)
+    d1[...] = near * r1[...] - deep * lt[...]
+    send_fields(1, d1)
+    send_backs(1, lambda at: near * (back_a[at] - alpha * back_c[at]) - deep * (back_b[at] - alpha * back_d[at]))
+    raw[...] = near * lt[...] - deep * (n0[...] - alpha * lz2[...])
+    halo_finish(raw, lambda d, kind: received(1, d, kind))
 
     columns = [dot_sum(z_field, raw), dot_sum(raw, r1), dot_sum(raw, raw), dot_sum(z_field, r1)]
     outs = [pltpu.make_async_copy(source, place_out, load_sem.at[k])
@@ -386,7 +331,7 @@
         for out in outs:
             out.start()
 
-    sums = mesh_sum(1, to_row(columns), (None, None, in_last_stage))
+    sums = mesh_sum(1, to_row(columns), (None, in_last_stage))
     cross, onto, square, kept = [from_row(sums, k) for k in range(4)]
     beta = cross / sum_zz
     alpha_b = (onto - beta * kept) / (square - beta * (2.0 * cross - beta * sum_zz))
@@ -396,12 +341,10 @@
 
     for out in outs:
         out.wait()
-    for around in range(6):
+    for around in range(2):
         for d in range(4):
             for kind in range(2):
                 halo_copy(around, d, kind).wait_send()
-    for copy in gram_copies():
-        copy.wait_send()
     for around in range(2):
         for index in range(len(STAGES)):
             for copy in sum_copies(around, index):
@@ -423,7 +366,7 @@
         field = EXT + (8, 64)
         vmem = pl.BlockSpec(memory_space=pltpu.VMEM)
         hbm = pl.BlockSpec(memory_space=pl.ANY)
-        fields = [pltpu.VMEM(EXT + (8, 128), F32)] * 15
+        fields = [pltpu.VMEM(EXT + (8, 128), F32)] * 14
         backs = [pltpu.VMEM(EXT + (8, 256), F32)] * 5
         parts = pl.pallas_call(
             functools.partial(on_device, sizes, row_len),
@@ -439,21 +382,17 @@
                 pltpu.VMEM(EXT + (8, 64), F32),
                 *backs,
                 *fields,
-                pltpu.VMEM((6, 2, 2, 16, 8, 128), BF16),
-                pltpu.VMEM((6, 2, 2, 8, 8, 128), BF16),
-                pltpu.VMEM((6, 2, 2, 16, 8, 128), BF16),
-                pltpu.VMEM((6, 2, 2, 8, 8, 128), BF16),
+                pltpu.VMEM((2, 2, 2, 16, 8, 128), BF16),
+                pltpu.VMEM((2, 2, 2, 8, 8, 128), BF16),
+                pltpu.VMEM((2, 2, 2, 16, 8, 128), BF16),
+                pltpu.VMEM((2, 2, 2, 8, 8, 128), BF16),
                 pltpu.VMEM((8, 1, 128), F32),
                 pltpu.VMEM((2 * SLOTS, 1, 128), F32),
-                pltpu.VMEM((1, 1, 128), F32),
-                pltpu.VMEM((8, 1, 128), F32),
                 pltpu.SemaphoreType.DMA((6,)),
-                pltpu.SemaphoreType.DMA((48,)),
-                pltpu.SemaphoreType.DMA((48,)),
+                pltpu.SemaphoreType.DMA((16,)),
+                pltpu.SemaphoreType.DMA((16,)),
                 pltpu.SemaphoreType.DMA((2 * SLOTS,)),
                 pltpu.SemaphoreType.DMA((2 * SLOTS,)),
-                pltpu.SemaphoreType.DMA((8,)),
-                pltpu.SemaphoreType.DMA((8,)),
             ],
             compiler_params=pltpu.CompilerParams(collective_id=0, has_side_effects=True),
         )(rhs[0], self_coupling[0], hopping[:, 0])

time: 87.6 us -> 86 us (0.982)
  Pallas kernels: 86.5 us -> 85.2 us
    pallas_call x1, Pallas kernels: 84.5 us -> 83.1 us  [step(): pl.pallas_call(functools.partial(on_device, sizes, row_len), out_shape=[j...]
where the time goes in v4:
time: 86 us; the launch traced here: 85.8 us
  Pallas kernels  85.2 us (99%)
    pallas_call x1, Pallas kernels, step(): pl.pallas_call(functools.partial(on_device, sizes, row_len), out_shape=[j...  83.1 us
    pallas_call x1, Pallas kernels, step(): pl.pallas_call(combine, out_shape=[jax.ShapeDtypeStruct(field, F32)] * 2,...  2.04 us

profile of v4, /device:TPU:1, one launch (start us, length us, event | category | flops | bytes accessed | tf_op | source)
XLA Modules:
  0.0 85.8 jit_solution(2995217829905163653)
XLA Ops:
  0.6 83.1 %shard_map.50 = (f32[2,2,4,4,8,128]{5,4,3,2,1,0:T(8,128)}, f32[2,2,4,4,8,128]{5,4,3,2,1,0:T(8,128)}, f32[2,2,4,4,8,128]{5,4,3,2,1,0:T(8,128)}, f32[2,8,128]{2,1,0:T(8,128)}) custom-call(f32[2,2,4,4,8,64]{5,4,3,2,1,0:T(8,128)} %bitcast.7, bf16[2,2,4,4,64,64]{5,4,3,2,1,0:T(8,128)(2,1)} %bitcast.6, bf16[4,2,2,4,4,64,64]{6,5,4,3,2,1,0:T(8,128)(2,1)} %bitcast.5), custom_call_target="tpu_custom_call" | custom-call | tf_op jit(solution)/shard_map/pallas_call | solution.py:371
  83.8 2.0 %shard_map.51 = (f32[2,2,4,4,8,64]{5,4,3,2,1,0:T(8,128)}, f32[2,2,4,4,8,64]{5,4,3,2,1,0:T(8,128)}) custom-call(f32[2,2,4,4,8,128]{5,4,3,2,1,0:T(8,128)} %get-tuple-element.8.pair_ref, f32[2,2,4,4,8,128]{5,4,3,2,1,0:T(8,128)} %get-tuple-element.9.zero_ref, f32[2,2,4,4,8,128]{5,4,3,2,1,0:T(8,128)} %get-tuple-element.10.left_ref, ...), custom_call_target="tpu_custom_call" | custom-call | tf_op jit(solution)/shard_map/pallas_call | solution.py:399

commit v5 on v2

--- a/solution.py
+++ b/solution.py
@@ -137,7 +137,7 @@
             out[x, y, z] = 4.0 * field[x, y, z] + (total + turned(total))
 
 
-def on_device(sizes, row_len, rhs_hbm, self_hbm, hop_hbm, sol_ref, res_ref,
+def on_device(sizes, row_len, rhs_hbm, self_hbm, hop_hbm, pair_out, zero_out, left_out, scale_out,
               rhs_in, links, hops, packed, split, ahead_sum, back_a, back_b, back_c, back_d, halo_in,
               rhs, m0, m1, r1, d0, z_field, rt, lt, lz, lt2, lz2, d1,
               send_xy, send_zt, got_xy, got_zt, rows_out, rows_in,
@@ -303,13 +303,25 @@
     halo_finish(1, lz)
 
     columns = [dot_sum(z_field, lz), dot_sum(lz, r1), dot_sum(lz, lz), dot_sum(z_field, r1)]
-    sums = mesh_sum(1, to_row(columns))
+    outs = [pltpu.make_async_copy(source, place_out, load_sem.at[k])
+            for k, (source, place_out) in enumerate(((rt, pair_out), (lt2, zero_out), (r1, left_out)))]
+
+    def in_last_stage():
+        rt[...] = jnp.where(lower, d0[...], d1[...])
+        lt2[...] = jnp.where(lower, z_field[...], lz[...])
+        for out in outs:
+            out.start()
+
+    sums = mesh_sum(1, to_row(columns), in_last_stage)
     cross, onto, square, kept = [from_row(sums, k) for k in range(4)]
     beta = cross / sum_zz
     alpha_b = (onto - beta * kept) / (square - beta * (2.0 * cross - beta * sum_zz))
-    sol_ref[...] = (alpha * d0[...] + alpha_b * (d1[...] - beta * d0[...]))[..., :64]
-    res_ref[...] = (r1[...] - alpha_b * (lz[...] - beta * z_field[...]))[..., :64]
-
+    half = lane_r < 64
+    scale_out[0] = jnp.where(half, alpha - alpha_b * beta, alpha_b)
+    scale_out[1] = jnp.where(half, alpha_b * beta, -alpha_b)
+
+    for out in outs:
+        out.wait()
     for around in range(2):
         for d in range(4):
             for kind in range(2):
@@ -319,6 +331,13 @@
                 copy.wait_send()
 
 
+def combine(pair_ref, zero_ref, left_ref, scale_ref, sol_ref, res_ref):
+    first = scale_ref[0] * pair_ref[...]
+    second = scale_ref[1] * zero_ref[...]
+    sol_ref[...] = (first + turned(first))[..., :64]
+    res_ref[...] = (left_ref[...] + (second + turned(second)))[..., :64]
+
+
 def solution(mesh):
     sizes = dict(mesh.shape)
     row_len = min(8, max(2, sizes["gx"] // 8))
@@ -329,11 +348,11 @@
         hbm = pl.BlockSpec(memory_space=pl.ANY)
         fields = [pltpu.VMEM(EXT + (8, 128), F32)] * 12
         backs = [pltpu.VMEM(EXT + (8, 256), F32)] * 5
-        sol, res = pl.pallas_call(
+        parts = pl.pallas_call(
             functools.partial(on_device, sizes, row_len),
-            out_shape=[jax.ShapeDtypeStruct(field, F32)] * 2,
+            out_shape=[jax.ShapeDtypeStruct(EXT + (8, 128), F32)] * 3 + [jax.ShapeDtypeStruct((2, 8, 128), F32)],
             in_specs=[hbm] * 3,
-            out_specs=[vmem] * 2,
+            out_specs=[hbm] * 3 + [vmem],
             scratch_shapes=[
                 pltpu.VMEM(field, F32),
                 pltpu.VMEM(EXT + (64, 64), BF16),
@@ -357,6 +376,12 @@
             ],
             compiler_params=pltpu.CompilerParams(collective_id=0, has_side_effects=True),
         )(rhs[0], self_coupling[0], hopping[:, 0])
+        sol, res = pl.pallas_call(
+            combine,
+            out_shape=[jax.ShapeDtypeStruct(field, F32)] * 2,
+            in_specs=[vmem] * 4,
+            out_specs=[vmem] * 2,
+        )(*parts)
         return sol[None], res[None]
 
     whole_spec = P("gx", None, None, "gz", "ta", None, None)

time: 85.1 us -> 83.5 us (0.981)
  local copies, waits for them, and re-layouts: 3.34 us -> 0 us
  Pallas kernels: 80.9 us -> 82.7 us
    unnamed x2 -> x0, local copies, waits for them, and re-layouts: 3.34 us -> none
    pallas_call x0 -> x1, Pallas kernels: none -> 2.04 us  [step(): pl.pallas_call(combine, out_shape=[jax.ShapeDtypeStruct(field, F32)] * 2,...]
where the time goes in v5:
time: 83.5 us; the launch traced here: 83.3 us
  Pallas kernels  82.7 us (99%)
    pallas_call x1, Pallas kernels, step(): pl.pallas_call(functools.partial(on_device, sizes, row_len), out_shape=[j...  80.6 us
    pallas_call x1, Pallas kernels, step(): pl.pallas_call(combine, out_shape=[jax.ShapeDtypeStruct(field, F32)] * 2,...  2.04 us

profile of v5, /device:TPU:1, one launch (start us, length us, event | category | flops | bytes accessed | tf_op | source)
XLA Modules:
  0.0 83.3 jit_solution(6117051753822028244)
XLA Ops:
  0.6 80.6 %shard_map.50 = (f32[2,2,4,4,8,128]{5,4,3,2,1,0:T(8,128)}, f32[2,2,4,4,8,128]{5,4,3,2,1,0:T(8,128)}, f32[2,2,4,4,8,128]{5,4,3,2,1,0:T(8,128)}, f32[2,8,128]{2,1,0:T(8,128)}) custom-call(f32[2,2,4,4,8,64]{5,4,3,2,1,0:T(8,128)} %bitcast.7, bf16[2,2,4,4,64,64]{5,4,3,2,1,0:T(8,128)(2,1)} %bitcast.6, bf16[4,2,2,4,4,64,64]{6,5,4,3,2,1,0:T(8,128)(2,1)} %bitcast.5), custom_call_target="tpu_custom_call" | custom-call | tf_op jit(solution)/shard_map/pallas_call | solution.py:351
  81.3 2.0 %shard_map.51 = (f32[2,2,4,4,8,64]{5,4,3,2,1,0:T(8,128)}, f32[2,2,4,4,8,64]{5,4,3,2,1,0:T(8,128)}) custom-call(f32[2,2,4,4,8,128]{5,4,3,2,1,0:T(8,128)} %get-tuple-element.8.pair_ref, f32[2,2,4,4,8,128]{5,4,3,2,1,0:T(8,128)} %get-tuple-element.9.zero_ref, f32[2,2,4,4,8,128]{5,4,3,2,1,0:T(8,128)} %get-tuple-element.10.left_ref, ...), custom_call_target="tpu_custom_call" | custom-call | tf_op jit(solution)/shard_map/pallas_call | solution.py:379
